TPU v7x, 512 devices: a whole 4x8x8 slice. The times are simulated.
512 devices in a mesh: group: 8 (over z), ray: 64 (over y, x, core).
Axes of the slice: x: 4, y: 8, z: 8, core: 2. Of those that a mesh axis runs over, the one named last changes fastest.
Arguments:
- bricks: bfloat16 [16384, 4096], P(('group', 'ray')), may hold values from -6 to 6
- work_bricks: int32 [8, 128], P('group', 'ray'), may hold values from 0 to 16383, as said below
- interp: bfloat16 [32768, 5, 512], P(('group', 'ray')), may hold values from 0 to 0.25
- tile_slot: int32 [32768, 5], P(('group', 'ray')), may hold values from 0 to 127, as said below
- spacing: float32 [32768, 40], P(('group', 'ray')), may hold values from 0.02 to 0.3
- targets: float32 [3, 32768], P(None, ('group', 'ray')), may hold values from 0 to 1
- weight_in: bfloat16 [64, 256], replicated, may hold values from -0.75 to 0.75
- weight_mid: bfloat16 [256, 256], replicated, may hold values from -0.375 to 0.375
- weight_out: bfloat16 [256, 4], replicated, may hold values from -0.375 to 0.375
Outputs:
- brick_grad: float32 [16384, 4096], P(('group', 'ray'))
Inputs may be any that keep to these rules, and one draw needn't show every extreme that they name: `work_bricks`: slot j of image group g is held by ray index j // 2 of the group, and its brick's owner, the device brick // 32 counted over group then ray, has that same ray index. Among the 2 slots of one device at most 2 name bricks owned in one image group, and on every device exactly 2 do for some group. `tile_slot`: of the 320 tiles of one device, at most 10 name slots held by one device of the group, and on every device some holder is named exactly 10 times.
All inputs are finite; a program needn't handle non-finite values.
Results may differ from a plain program's by a relative error of at most 0.0022.
Values may be sent and summed in bfloat16 or wider, within the bound.
A program may use at most 64 MiB of HBM per device.

v0:
```python
import jax
import jax.numpy as jnp
from jax import lax
from jax.sharding import PartitionSpec as P


def silu_slope(pre_act):
    logistic = jax.nn.sigmoid(pre_act)
    return logistic * (1.0 + pre_act * (1.0 - logistic))


def composite_loss(raw_out, spacing, targets):
    density = jax.nn.softplus(raw_out[:, :, 0])
    shading = jax.nn.sigmoid(raw_out[:, :, 1:4])
    optical = density * spacing
    before_sum = jnp.cumsum(optical, axis=1) - optical
    ray_weight = jnp.exp(-before_sum) * (1.0 - jnp.exp(-optical))
    colour = jnp.sum(ray_weight[:, :, None] * shading, axis=1)
    return 0.5 * jnp.sum((colour - targets.T) ** 2)


def feature_grad(features, spacing, targets, weight_in, weight_mid, weight_out):
    pre_first = jnp.dot(features, weight_in, preferred_element_type=jnp.float32)
    act_first = jax.nn.silu(pre_first).astype(jnp.bfloat16)
    pre_second = jnp.dot(act_first, weight_mid, preferred_element_type=jnp.float32)
    act_second = jax.nn.silu(pre_second).astype(jnp.bfloat16)
    raw_out = jnp.dot(act_second, weight_out, preferred_element_type=jnp.float32)
    ray_count = spacing.shape[0]
    raw_grad = jax.grad(composite_loss)(raw_out.reshape(ray_count, -1, 4), spacing, targets)
    raw_grad = raw_grad.reshape(-1, 4).astype(jnp.bfloat16)
    grad_second = jnp.dot(raw_grad, weight_out.T, preferred_element_type=jnp.float32)
    slope_second = (grad_second * silu_slope(pre_second)).astype(jnp.bfloat16)
    grad_first = jnp.dot(slope_second, weight_mid.T, preferred_element_type=jnp.float32)
    slope_first = (grad_first * silu_slope(pre_first)).astype(jnp.bfloat16)
    return jnp.dot(slope_first, weight_in.T, preferred_element_type=jnp.float32).astype(
        jnp.bfloat16
    )


def earlier_equal(labels):
    order_index = jnp.arange(labels.shape[0])
    matches = (labels[:, None] == labels[None, :]) & (order_index[None, :] < order_index[:, None])
    return jnp.sum(matches.astype(jnp.int32), axis=1)


def per_device(
    bricks, work_bricks, interp, tile_slot, spacing, targets, weight_in, weight_mid, weight_out
):
    own_count = bricks.shape[0]
    row_width = bricks.shape[1]
    held_count = work_bricks.shape[1]
    channels = weight_in.shape[0]
    voxels = row_width // channels
    rays_dev, segments, span = interp.shape
    samples = span // voxels
    tiles_dev = rays_dev * segments
    group_size = lax.axis_size("group")
    ray_size = lax.axis_size("ray")
    per_owner = 1 + (held_count + group_size - 2) // group_size
    entries = work_bricks[0]
    owner_group = entries // own_count // ray_size
    local_id = entries % own_count
    entry_rank = earlier_equal(owner_group)
    requests = (
        jnp.full((group_size, per_owner), -1, jnp.int32).at[owner_group, entry_rank].set(local_id)
    )
    asked = lax.all_to_all(requests, "group", split_axis=0, concat_axis=0, tiled=True)
    wanted = asked >= 0
    picked = jnp.take(bricks, jnp.where(wanted, asked, 0).reshape(-1), axis=0)
    picked = jnp.where(
        wanted[:, :, None],
        picked.reshape(group_size, per_owner, row_width),
        jnp.zeros((), jnp.bfloat16),
    )
    fetched = lax.all_to_all(picked, "group", split_axis=0, concat_axis=0, tiled=True)
    holdings = fetched[owner_group, entry_rank]
    group_set = lax.all_gather(holdings, "ray", axis=0, tiled=True)
    weights_tiles = interp.reshape(tiles_dev, samples, voxels)
    slots = tile_slot.reshape(-1)
    tiles = jnp.take(group_set, slots, axis=0).reshape(tiles_dev, voxels, channels)
    made = jnp.einsum("tiv,tvc->tic", weights_tiles, tiles, preferred_element_type=jnp.float32)
    features = made.astype(jnp.bfloat16).reshape(-1, channels)
    tile_gradients = feature_grad(features, spacing, targets, weight_in, weight_mid, weight_out)
    grads_tiles = tile_gradients.reshape(tiles_dev, samples, channels)
    outer = jnp.einsum(
        "tiv,tic->tvc", weights_tiles, grads_tiles, preferred_element_type=jnp.float32
    )
    group_grad = jax.ops.segment_sum(
        outer.reshape(tiles_dev, row_width), slots, num_segments=held_count * ray_size
    )
    slot_grad = lax.psum_scatter(group_grad, "ray", scatter_dimension=0, tiled=True)
    outgoing = (
        jnp.zeros((group_size, per_owner, row_width), jnp.float32)
        .at[owner_group, entry_rank]
        .set(slot_grad)
    )
    arrived = lax.all_to_all(outgoing, "group", split_axis=0, concat_axis=0, tiled=True).reshape(
        group_size * per_owner, row_width
    )
    destination = jnp.where(wanted, asked, own_count).reshape(-1)
    return jax.ops.segment_sum(arrived, destination, num_segments=own_count + 1)[:own_count]


def solution(mesh):
    in_specs = (
        P(("group", "ray"), None),
        P("group", "ray"),
        P(("group", "ray"), None, None),
        P(("group", "ray"), None),
        P(("group", "ray"), None),
        P(None, ("group", "ray")),
        P(),
        P(),
        P(),
    )
    out_specs = P(("group", "ray"), None)
    return jax.shard_map(
        per_device, mesh=mesh, in_specs=in_specs, out_specs=out_specs, check_vma=False
    )
```

profile of v0, /device:TPU:1, one launch (start us, length us, event | category | flops | bytes accessed | tf_op | source)
XLA Modules:
  0.0 435.2 jit_solution(10257369317479114690)
XLA Ops:
  9.6 17.2 %all_to_all.25 = s32[8,1,2]{2,1,0:T(1,128)S(1)} all-to-all(s32[8,1,2]{2,1,0:T(1,128)S(1)} %copy.55), channel_id=1, replica_groups=mesh['group'=8,'ray'=64] {'group'}, dimensions={0} | all-to-all | bytes 128 | tf_op jit(solution)/shard_map/all_to_all | solution.py:67
  29.8 10.4 %all_to_all.26 = bf16[8,2,4096]{2,1,0:T(2,128)(2,1)S(1)} all-to-all(bf16[8,2,4096]{2,1,0:T(2,128)(2,1)S(1)} %broadcast_select_fusion.2), channel_id=1, replica_groups=mesh['group'=8,'ray'=64] {'group'}, dimensions={0} | all-to-all | bytes 262144 | tf_op jit(solution)/shard_map/all_to_all | solution.py:75
  40.2 1.2 gather_fusion.1
  42.1 1.3 reshape.277
  44.2 78.5 %all-gather.3.cloned.1.call-done = bf16[64,2,4096]{2,1,0:T(2,128)(2,1)} async-done(((bf16[1,2,4096]{2,1,0:T(2,128)(2,1)}), bf16[64,2,4096]{2,1,0:T(2,128)(2,1)}) %all-gather.3.cloned.1.call-update) | async-done | bytes 1048592 | tf_op jit(solution)/shard_map/all_gather | solution.py:77
  122.7 1.5 reshape.335
  124.1 3.9 gather_fusion.2
  128.0 3.3 copy.61
  131.3 2.0 broadcast_select_fusion
  133.3 10.1 %copy.63 = bf16[320,64,64]{2,1,0:T(8,128)(2,1)} copy(bf16[320,64,64]{0,2,1:T(8,128)(2,1)} %broadcast_select_fusion) | data formatting | bytes 5242880 | tf_op jit(solution)/shard_map/jit(_take)/select_n | solution.py:80
  143.4 4.3 fusion.8
  147.8 1.7 fusion.4
  149.5 1.5 copy-done.8
  151.0 1.4 fusion.5
  152.4 1.6 reshape.279
  154.0 1.4 fusion.20
  155.4 1.6 reduce_window_sum.22
  158.8 1.6 fusion.12
  161.0 1.4 fusion.21
  162.4 1.6 reduce_window_sum.23
  164.9 1.5 add_convert_fusion
  166.5 1.6 convert_element_type.36
  168.1 4.0 fusion
  172.0 3.3 convolution_convert_fusion
  175.3 1.3 copy.66
  176.6 4.9 %convolution_bitcast_fusion = f32[320,64,64]{1,2,0:T(8,128)} fusion(bf16[320,8,64]{2,1,0:T(8,128)(2,1)S(1)} %copy-done.1, bf16[2560,64]{1,0:T(8,128)(2,1)S(1)} %copy.66), kind=kOutput, calls=%fused_computation.11 | convolution fusion | flops 20971520 | bytes 5898240 | tf_op jit(solution)/shard_map/tiv,tic->tvc/dot_general | solution.py:85
  181.5 11.8 %copy.67 = f32[320,64,64]{0,2,1:T(8,128)} copy(f32[320,64,64]{1,2,0:T(8,128)} %convolution_bitcast_fusion) | data formatting | bytes 10485760 | tf_op jit(solution)/shard_map/tiv,tic->tvc/dot_general | solution.py:85
  193.4 6.2 %copy.68 = f32[320,4096]{1,0:T(8,128)} copy(f32[320,4096]{0,1:T(8,128)} %bitcast.97) | data formatting | bytes 10485760 | tf_op jit(solution)/shard_map/reshape | solution.py:89
  199.6 10.6 %scatter_custom_fusion.1 = f32[128,4096]{1,0:T(8,128)} fusion(s32[320]{0:T(512)S(1)} %reshape.313, f32[320,4096]{1,0:T(8,128)} %copy.68, f32[]{:T(128)} %constant.85.clone.1), kind=kCustom, calls=%fused_computation.23 | custom fusion | flops 1310720 | bytes 2097664 | tf_op jit(solution)/shard_map/scatter-add | solution.py:88
  210.2 1.3 dynamic-slice
  212.1 195.9 %all-reduce.5.cloned.1.call-done = f32[128,4096]{1,0:T(8,128)} async-done(((f32[128,4096]{1,0:T(8,128)}), f32[128,4096]{1,0:T(8,128)}) %all-reduce.5.cloned.1.call-update) | async-done | bytes 2097168
  409.8 16.3 %all_to_all.27 = f32[8,2,4096]{2,1,0:T(2,128)S(1)} all-to-all(f32[8,2,4096]{2,1,0:T(2,128)S(1)} %scatter_fusion.1), channel_id=1, replica_groups=mesh['group'=8,'ray'=64] {'group'}, dimensions={0} | all-to-all | bytes 524288 | tf_op jit(solution)/shard_map/all_to_all | solution.py:97
  (59 shorter events, 14.7 us)
Async XLA Ops:
  6.5 22.0 %copy-start = (bf16[32,4096]{1,0:T(8,128)(2,1)S(1)}, bf16[32,4096]{1,0:T(8,128)(2,1)}, u32[]{:S(2)}) copy-start(bf16[32,4096]{1,0:T(8,128)(2,1)} %param.9) | copy-start | bytes 786436
  6.5 35.0 %copy-start.5 = (s32[64,5]{0,1:T(8,128)S(1)}, s32[64,5]{0,1:T(8,128)}, u32[]{:S(2)}) copy-start(s32[64,5]{0,1:T(8,128)} %param.12) | copy-start | bytes 3844
  6.5 35.4 %copy-start.2 = (bf16[64,5,512]{2,0,1:T(8,128)(2,1)S(1)}, bf16[64,5,512]{2,0,1:T(8,128)(2,1)}, u32[]{:S(2)}) copy-start(bf16[64,5,512]{2,0,1:T(8,128)(2,1)} %param.11) | copy-start | bytes 983044
  6.5 116.1 %all-gather.3.cloned.1.call-start = ((), (), s32[]{:S(2)}) async-start(), calls=%async_computation.3 | async-start | bytes 1064960 | tf_op jit(solution)/shard_map/all_gather | solution.py:77
  8.8 34.6 %copy-start.4 = (f32[64,40]{0,1:T(8,128)S(1)}, f32[64,40]{0,1:T(8,128)}, u32[]{:S(2)}) copy-start(f32[64,40]{0,1:T(8,128)} %param.13) | copy-start | bytes 30724
  41.5 366.6 %all-reduce.5.cloned.1.call-start = ((), (), s32[]{:S(2)}) async-start(), calls=%async_computation.4 | async-start | bytes 4194304
  133.3 10.1 %copy-start.1 = (bf16[320,8,64]{2,1,0:T(8,128)(2,1)S(1)}, bf16[320,8,64]{2,1,0:T(8,128)(2,1)}, u32[]{:S(2)}) copy-start(bf16[320,8,64]{2,1,0:T(8,128)(2,1)} %reshape.277) | copy-start | bytes 983044
  147.7 3.3 copy-start.7
  149.5 1.5 copy-start.8
  151.0 7.8 %copy-start.6 = (f32[3,64]{1,0:T(4,128)S(1)}, f32[3,64]{1,0:T(4,128)}, u32[]{:S(2)}) copy-start(f32[3,64]{1,0:T(4,128)} %param.14) | copy-start | bytes 2308
  160.4 0.6 copy-start.3
Sparse Core Ops, SparseCore 0:
  41.6 80.9 all-gather.2
  210.3 197.6 all-reduce.4
where the time goes:
time: 439 us; the launch traced here: 435 us
  waiting for transfers between devices  274 us (62%)
  local copies, waits for them, and re-layouts  53.5 us (12%)
  blocking collectives  43.9 us (10%)
  other arithmetic  29.4 us (7%)
  matrix products  19.6 us (4%)
  between operations  14.3 us (3%)
    unnamed x3, waiting for transfers between devices  196 us
    all_gather x1, waiting for transfers between devices, per_device(): group_set = lax.all_gather(holdings, 'ray', axis=0, tiled=True)  78.5 us
    all_to_all x1, blocking collectives, per_device(): lax.all_to_all(requests, 'group', split_axis=0, concat_axis=0, tiled=True)  17.2 us
    all_to_all x1, blocking collectives, per_device(): lax.all_to_all(outgoing, 'group', split_axis=0, concat_axis=0, tiled=True)  16.3 us
    dot_general x1, local copies, waits for them, and re-layouts, per_device(): jnp.einsum('tiv,tic->tvc', weights_tiles, grads_tiles, preferred_element_...  11.8 us
    scatter-add x1, other arithmetic, per_device(): jax.ops.segment_sum(outer.reshape(tiles_dev, row_width), slots, num_segme...  10.6 us
    all_to_all x1, blocking collectives, per_device(): lax.all_to_all(picked, 'group', split_axis=0, concat_axis=0, tiled=True)  10.4 us
    select_n x1, local copies, waits for them, and re-layouts, per_device(): jnp.take(group_set, slots, axis=0).reshape(tiles_dev, voxels, channels)  10.1 us
  transfers between devices with their start and end apart: 2, of which 2 were waited for; matrix products, arithmetic and copies ran while one was open for 1% of the time, Pallas kernels for 0%

commit v1 on v0

v1 whole, which is shorter than its diff:
```python
import functools

import jax
import jax.numpy as jnp
from jax import lax
from jax.experimental import pallas as pl
from jax.experimental.pallas import tpu as pltpu
from jax.sharding import PartitionSpec as P

MESH = pl.DeviceIdType.MESH
F32 = jnp.float32
BF16 = jnp.bfloat16
NX = 4
NC = 2
HIGHEST = lax.Precision.HIGHEST


def coordinates():
    ray = lax.axis_index("ray")
    return ray // (NX * NC), (ray // NC) % NX, ray % NC


def ray_of(y, x, c):
    return (y * NX + x) * NC + c


class Peers:
    def __init__(self, nz, ny):
        self.nz, self.ny = nz, ny
        self.z = lax.axis_index("group")
        self.y, self.x, self.c = coordinates()

    def along_z(self, d):
        return {"group": lax.rem(self.z + d, self.nz)}

    def along_y(self, d):
        return {"ray": ray_of(lax.rem(self.y + d, self.ny), self.x, self.c)}

    def along_x(self, d):
        return {"ray": ray_of(self.y, lax.rem(self.x + d, NX), self.c)}

    def partner(self):
        return {"ray": ray_of(self.y, self.x, 1 - self.c)}

    def everybody(self):
        out = [self.along_z(d) for d in range(1, self.nz)]
        out += [self.along_y(d) for d in range(1, self.ny)]
        return out + [self.along_x(1), self.along_x(NX - 1), self.partner()]

    def barrier(self):
        sem = pltpu.get_barrier_semaphore()
        peers = self.everybody()
        for peer in peers:
            pl.semaphore_signal(sem, inc=1, device_id=peer, device_id_type=MESH)
        pl.semaphore_wait(sem, len(peers))


class Copies:
    def __init__(self, send_sems, recv_sems):
        self.send_sems, self.recv_sems, self.count, self.live = send_sems, recv_sems, 0, []

    def make(self, src, dst, device):
        at = self.count
        self.count += 1
        copy = pltpu.make_async_remote_copy(
            src_ref=src,
            dst_ref=dst,
            send_sem=self.send_sems.at[at],
            recv_sem=self.recv_sems.at[at],
            device_id=device,
            device_id_type=MESH,
        )
        self.live.append(copy)
        return copy

    def start(self, src, dst, device):
        copy = self.make(src, dst, device)
        copy.start()
        return copy

    def drain(self):
        for copy in self.live:
            copy.wait_send()


def near_first(n):
    out = []
    for d in range(1, n // 2 + 1):
        out.append(d)
        if n - d != d:
            out.append(n - d)
    return out


def fetch_copies(nz, ny):
    return 2 * (nz - 1) + (ny - 1) + 3 * ny + 4 * ny


def fetch_kernel(
    nz, ny, wb_ref, bricks_ref, gs_ref, reqs_ref, mine, picks, sendb, arrived, send_sems, recv_sems
):
    peers = Peers(nz, ny)
    copies = Copies(send_sems, recv_sems)
    own_count = bricks_ref.shape[0]
    row = lax.broadcasted_iota(jnp.int32, mine.shape, 0)
    tile = jnp.where(row == 0, wb_ref[0, 0], wb_ref[0, 1])
    mine[...] = tile
    reqs_ref[0] = tile
    peers.barrier()
    asks = [
        copies.start(mine, reqs_ref.at[nz - d], peers.along_z(d)) for d in near_first(nz)
    ]
    for ask in asks:
        ask.wait_recv()
    base = (lax.axis_index("group") * lax.axis_size("ray") + lax.axis_index("ray")) * own_count
    lane = lax.broadcasted_iota(jnp.int32, (nz, 128), 1)
    rows = []
    for s in range(2):
        ids = jnp.concatenate([reqs_ref[e, s : s + 1, :] for e in range(nz)], axis=0)
        rows.append(jnp.where(ids - base == lane, 1.0, 0.0).astype(F32))
    choose = jnp.concatenate(rows, axis=0)[:, :own_count].astype(BF16)
    picked = jnp.dot(choose, bricks_ref[...], preferred_element_type=F32)
    for s in range(2):
        for p in range(32):
            picks[pl.ds(s * 32 + p, nz, stride=64), :] = picked[
                s * nz : (s + 1) * nz, p * 128 : (p + 1) * 128
            ]
    sendb[...] = picks[...].reshape(nz, 2, 32, 128).astype(BF16)
    gives = [
        copies.start(sendb.at[d], arrived.at[nz - d], peers.along_z(d)) for d in near_first(nz)
    ]
    held = sendb[0].astype(F32)
    for d, give in zip(near_first(nz), gives):
        give.wait_recv()
        held = held + arrived[nz - d].astype(F32)
    gs_ref[0, 0, 0] = held.astype(BF16)
    spread = {
        ny - d: copies.start(gs_ref.at[0, 0, 0], gs_ref.at[0, 0, ny - d], peers.along_y(d))
        for d in near_first(ny)
    }
    order = [0] + [ny - d for d in near_first(ny)]
    right, left, partner = peers.along_x(1), peers.along_x(NX - 1), peers.partner()
    from_left, from_right, cores = {}, {}, []
    for e in order:
        if e:
            spread[e].wait_recv()
        block = gs_ref.at[0, 0, e]
        from_left[e] = copies.start(block, gs_ref.at[0, 3, e], right)
        from_right[e] = copies.start(block, gs_ref.at[0, 1, e], left)
        cores.append(copies.start(block, gs_ref.at[1, 0, e], partner))
    relays = {}
    for n, e in enumerate(order):
        from_left[e].wait_recv()
        if n % 2 == 0:
            relays[e] = copies.start(gs_ref.at[0, 3, e], gs_ref.at[0, 2, e], right)
        cores.append(copies.start(gs_ref.at[0, 3, e], gs_ref.at[1, 3, e], partner))
        from_right[e].wait_recv()
        if n % 2 == 1:
            relays[e] = copies.start(gs_ref.at[0, 1, e], gs_ref.at[0, 2, e], left)
        cores.append(copies.start(gs_ref.at[0, 1, e], gs_ref.at[1, 1, e], partner))
    for e in order:
        relays[e].wait_recv()
        cores.append(copies.start(gs_ref.at[0, 2, e], gs_ref.at[1, 2, e], partner))
    for copy in cores:
        copy.wait_recv()
    copies.drain()


def fetch(nz, ny, work_bricks, bricks):
    total = fetch_copies(nz, ny)
    vmem = pl.BlockSpec(memory_space=pltpu.VMEM)
    return pl.pallas_call(
        functools.partial(fetch_kernel, nz, ny),
        out_shape=(
            jax.ShapeDtypeStruct((2, NX, ny, 2, 32, 128), BF16),
            jax.ShapeDtypeStruct((nz, 8, 128), jnp.int32),
        ),
        in_specs=[pl.BlockSpec(memory_space=pltpu.SMEM), vmem],
        out_specs=(vmem, vmem),
        scratch_shapes=[
            pltpu.VMEM((8, 128), jnp.int32),
            pltpu.VMEM((nz * 64, 128), F32),
            pltpu.VMEM((nz, 2, 32, 128), BF16),
            pltpu.VMEM((nz, 2, 32, 128), BF16),
            pltpu.SemaphoreType.DMA((total,)),
            pltpu.SemaphoreType.DMA((total,)),
        ],
        compiler_params=pltpu.CompilerParams(collective_id=0, has_side_effects=True),
        name="fetch",
    )(work_bricks, bricks)


def reduce_kernel(
    nz,
    ny,
    acc_ref,
    zout_ref,
    cbuf,
    part,
    relay_a,
    relay_b,
    from_left,
    from_right,
    ybuf,
    send_sems,
    recv_sems,
):
    peers = Peers(nz, ny)
    copies = Copies(send_sems, recv_sems)
    half = ny // 2
    a, b = pl.ds(0, half), pl.ds(half, half)
    right, left, partner = peers.along_x(1), peers.along_x(NX - 1), peers.partner()
    peers.barrier()
    core = {j: copies.start(acc_ref.at[1, j], cbuf.at[j], partner) for j in (2, 1, 3, 0)}

    def merge(j):
        core[j].wait_recv()
        part[j] = acc_ref[0, j] + cbuf[j]

    merge(2)
    far_a = copies.start(part.at[2, a], relay_a, right)
    far_b = copies.start(part.at[2, b], relay_b, left)
    merge(1)
    left_b = copies.start(part.at[1, b], from_left.at[b], right)
    merge(3)
    right_a = copies.start(part.at[3, a], from_right.at[a], left)
    far_a.wait_recv()
    part[1, a] = part[1, a] + relay_a[...]
    left_a = copies.start(part.at[1, a], from_left.at[a], right)
    far_b.wait_recv()
    part[3, b] = part[3, b] + relay_b[...]
    right_b = copies.start(part.at[3, b], from_right.at[b], left)
    merge(0)
    ys = {}
    right_a.wait_recv()
    left_a.wait_recv()
    part[0, a] = part[0, a] + from_left[a] + from_right[a]
    for e in range(1, half):
        ys[e] = copies.start(part.at[0, e], ybuf.at[ny - e], peers.along_y(e))
    left_b.wait_recv()
    right_b.wait_recv()
    part[0, b] = part[0, b] + from_left[b] + from_right[b]
    for e in range(half, ny):
        ys[e] = copies.start(part.at[0, e], ybuf.at[ny - e], peers.along_y(e))
    mine = part[0, 0]
    for e in range(1, ny):
        ys[e].wait_recv()
        mine = mine + ybuf[ny - e]
    zout_ref[0] = mine
    zs = [copies.start(zout_ref.at[0], zout_ref.at[nz - d], peers.along_z(d)) for d in near_first(nz)]
    for copy in zs:
        copy.wait_recv()
    copies.drain()


def reduce_plane(nz, ny, acc):
    total = 4 + 6 + (ny - 1) + (nz - 1)
    vmem = pl.BlockSpec(memory_space=pltpu.VMEM)
    half = (ny // 2, 2, 32, 128)
    whole = (ny, 2, 32, 128)
    return pl.pallas_call(
        functools.partial(reduce_kernel, nz, ny),
        out_shape=jax.ShapeDtypeStruct((nz, 2, 32, 128), F32),
        in_specs=[vmem],
        out_specs=vmem,
        scratch_shapes=[
            pltpu.VMEM((NX,) + whole, F32),
            pltpu.VMEM((NX,) + whole, F32),
            pltpu.VMEM(half, F32),
            pltpu.VMEM(half, F32),
            pltpu.VMEM(whole, F32),
            pltpu.VMEM(whole, F32),
            pltpu.VMEM(whole, F32),
            pltpu.SemaphoreType.DMA((total,)),
            pltpu.SemaphoreType.DMA((total,)),
        ],
        compiler_params=pltpu.CompilerParams(collective_id=1, has_side_effects=True),
        name="reduce_plane",
    )(acc)


def place_kernel(base_ref, reqs_ref, z_ref, out_ref):
    nz = reqs_ref.shape[0]
    own_count = out_ref.shape[0]
    lane = lax.broadcasted_iota(jnp.int32, (2 * nz, 128), 1)
    ids = jnp.concatenate([reqs_ref[e, 0:2, :] for e in range(nz)], axis=0)
    hit = jnp.where(ids - base_ref[0] == lane, 1.0, 0.0).astype(F32)
    spread = jnp.transpose(hit)[:own_count]
    for p in range(32):
        rows = z_ref[pl.ds(p, 2 * nz, stride=32), :]
        out_ref[:, p * 128 : (p + 1) * 128] = jnp.dot(
            spread, rows, precision=HIGHEST, preferred_element_type=F32
        )


def place(own_count, base, reqs, zout):
    vmem = pl.BlockSpec(memory_space=pltpu.VMEM)
    return pl.pallas_call(
        place_kernel,
        out_shape=jax.ShapeDtypeStruct((own_count, 4096), F32),
        in_specs=[pl.BlockSpec(memory_space=pltpu.SMEM), vmem, vmem],
        out_specs=vmem,
        name="place",
    )(base, reqs, zout.reshape(-1, 128))


def logistic(x):
    return 0.5 * jnp.tanh(0.5 * x) + 0.5


def compute_kernel(
    slots_ref,
    interp_ref,
    gs_ref,
    spacing_ref,
    targets_ref,
    win_ref,
    wmid_ref,
    wout_ref,
    acc_ref,
    wc,
    feat_a,
    feat_b,
    slope_a,
    slope_b,
    raw_s,
    grad_s,
    gfeat,
):
    segs, rays, _ = interp_ref.shape
    chunk = rays * 8
    steps = segs * 8
    unroll = 16

    src = lax.broadcasted_iota(jnp.int32, (128, 512), 0)
    dst = lax.broadcasted_iota(jnp.int32, (128, 512), 1)
    voxel = src % 64
    perm = jnp.where(
        (dst // 128 == (src // 64) * 2 + voxel % 2) & (dst % 128 == voxel // 2), 1.0, 0.0
    ).astype(BF16)
    for seg in range(segs):
        for j in range(4):
            moved = jnp.dot(
                interp_ref[seg, :, j * 128 : (j + 1) * 128], perm, preferred_element_type=F32
            )
            for i2 in range(2):
                for h in range(2):
                    blk = i2 * 2 + h
                    wc[pl.ds(seg * rays * 16 + h * 8 + 2 * j + i2, rays, stride=16), :] = moved[
                        :, blk * 128 : (blk + 1) * 128
                    ]
    acc_ref[...] = jnp.zeros_like(acc_ref)

    def tile_weights(tile):
        return wc[pl.ds(pl.multiple_of(tile * 16, 16), 16), :][:, :32].astype(BF16)

    win = win_ref[...]
    wmid = wmid_ref[...]
    wout = jnp.concatenate([wout_ref[...].astype(F32), jnp.zeros((4, 256), F32)], axis=0).astype(BF16)
    win_wide = jnp.concatenate([win.astype(F32), jnp.zeros((64, 256), F32)], axis=0).astype(BF16)

    for seg in range(segs):

        @pl.loop(0, rays // unroll)
        def _(group):
            for u in range(unroll):
                r = group * unroll + u
                brick = gs_ref[slots_ref[seg, r]]
                made = jnp.dot(tile_weights(seg * rays + r), brick, preferred_element_type=F32)
                feat_a[pl.ds(r, 8, stride=rays), :] = made[:8]
                feat_b[pl.ds(r, 8, stride=rays), :] = made[8:]

        rows = pl.ds(seg * chunk, chunk)
        features = (feat_a[...] + pltpu.roll(feat_b[...], 64, 1))[:, :64].astype(BF16)
        pre = jnp.dot(features, win, preferred_element_type=F32)
        s = logistic(pre)
        act = pre * s
        slope_a[rows, :] = s * (1.0 + (pre - act))
        pre = jnp.dot(act.astype(BF16), wmid, preferred_element_type=F32)
        s = logistic(pre)
        act = pre * s
        slope_b[rows, :] = s * (1.0 + (pre - act))
        raw = lax.dot_general(
            wout, act.astype(BF16), (((1,), (1,)), ((), ())), preferred_element_type=F32
        )
        turned = pltpu.roll(raw, chunk - rays, 1)
        for i in range(0, 8, 2):
            at = i * rays
            raw_s[pl.ds(seg * 8 + i, 8, stride=steps), :] = raw[:, at : at + 128]
            raw_s[pl.ds(seg * 8 + i + 1, 8, stride=steps), :] = turned[:, at : at + 128]

    spacing = spacing_ref[...]
    k0 = lax.broadcasted_iota(jnp.int32, (steps, steps), 0)
    k1 = lax.broadcasted_iota(jnp.int32, (steps, steps), 1)
    earlier = jnp.where(k1 < k0, 1.0, 0.0).astype(F32)
    later = jnp.where(k1 > k0, 1.0, 0.0).astype(F32)
    raw0 = raw_s[0:steps, :][:, :rays]
    density = jnp.maximum(raw0, 0.0) + jnp.log1p(jnp.exp(-jnp.abs(raw0)))
    optical = density * spacing
    before = jnp.dot(earlier, optical, precision=HIGHEST, preferred_element_type=F32)
    through = jnp.exp(-before)
    kept = jnp.exp(-optical)
    weight = through * (1.0 - kept)
    pull = jnp.zeros_like(weight)
    grads = []
    for ch in range(3):
        shade = logistic(raw_s[(ch + 1) * steps : (ch + 2) * steps, :][:, :rays])
        colour = jnp.sum(weight * shade, axis=0, keepdims=True)
        err = colour - targets_ref[ch : ch + 1, :]
        pull = pull + err * shade
        grads.append(err * weight * shade * (1.0 - shade))
    after = jnp.dot(later, pull * weight, precision=HIGHEST, preferred_element_type=F32)
    grads.insert(0, (pull * through * kept - after) * spacing * logistic(raw0))
    grad_s[...] = jnp.zeros_like(grad_s)
    for ch in range(4):
        grad_s[ch * steps : (ch + 1) * steps, :rays] = grads[ch]

    for seg in range(segs):
        pieces = []
        for i in range(0, 8, 2):
            even = grad_s[pl.ds(seg * 8 + i, 8, stride=steps), :]
            odd = grad_s[pl.ds(seg * 8 + i + 1, 8, stride=steps), :]
            pieces.append(even + pltpu.roll(odd, rays, 1))
        raw_grad = jnp.concatenate(pieces, axis=1).astype(BF16)
        rows = pl.ds(seg * chunk, chunk)
        grad = lax.dot_general(
            raw_grad, wout, (((0,), (0,)), ((), ())), preferred_element_type=F32
        )
        slope = (grad * slope_b[rows, :]).astype(BF16)
        grad = lax.dot_general(slope, wmid, (((1,), (1,)), ((), ())), preferred_element_type=F32)
        slope = (grad * slope_a[rows, :]).astype(BF16)
        grad = lax.dot_general(
            slope, win_wide, (((1,), (1,)), ((), ())), preferred_element_type=F32
        )
        gfeat[...] = grad.astype(BF16).astype(F32)

        @pl.loop(0, rays // unroll)
        def _(group):
            for u in range(unroll):
                r = group * unroll + u
                g = gfeat[pl.ds(r, 8, stride=rays), :]
                both = jnp.concatenate([g, pltpu.roll(g, 64, 1)], axis=0).astype(BF16)
                outer = lax.dot_general(
                    tile_weights(seg * rays + r),
                    both,
                    (((0,), (0,)), ((), ())),
                    preferred_element_type=F32,
                )
                slot = slots_ref[seg, r]
                acc_ref[slot] = acc_ref[slot] + outer


def compute(slots, interp, gs, spacing, targets, weight_in, weight_mid, weight_out):
    segs, rays, _ = interp.shape
    tiles, samples = segs * rays, segs * rays * 8
    vmem = pl.BlockSpec(memory_space=pltpu.VMEM)
    return pl.pallas_call(
        compute_kernel,
        out_shape=jax.ShapeDtypeStruct(gs.shape, F32),
        in_specs=[pl.BlockSpec(memory_space=pltpu.SMEM)] + [vmem] * 7,
        out_specs=vmem,
        scratch_shapes=[
            pltpu.VMEM((tiles * 16, 128), F32),
            pltpu.VMEM((rays * 8, 128), F32),
            pltpu.VMEM((rays * 8, 128), F32),
            pltpu.VMEM((samples, 256), F32),
            pltpu.VMEM((samples, 256), F32),
            pltpu.VMEM((8 * segs * 8, 128), F32),
            pltpu.VMEM((8 * segs * 8, 128), F32),
            pltpu.VMEM((rays * 8, 128), F32),
        ],
        compiler_params=pltpu.CompilerParams(vmem_limit_bytes=50 * 2**20),
        name="compute",
    )(slots, interp, gs, spacing, targets, weight_in, weight_mid, weight_out)


def per_device(
    bricks, work_bricks, interp, tile_slot, spacing, targets, weight_in, weight_mid, weight_out
):
    nz = lax.axis_size("group")
    ny = lax.axis_size("ray") // (NX * NC)
    y, x, c = coordinates()
    slot = tile_slot.T
    holder = slot // 2
    rel_y = (holder // (NX * NC) - y + ny) % ny
    rel_x = ((holder // NC) % NX - x + NX) % NX
    rel_c = jnp.abs(holder % NC - c)
    slots = ((rel_c * NX + rel_x) * ny + rel_y) * 2 + slot % 2
    own_count = bricks.shape[0]
    base = (lax.axis_index("group") * lax.axis_size("ray") + lax.axis_index("ray")) * own_count
    gs, reqs = fetch(nz, ny, work_bricks, bricks)
    acc = compute(
        slots,
        interp.transpose(1, 0, 2),
        gs.reshape(-1, 32, 128),
        spacing.T,
        targets,
        weight_in,
        weight_mid,
        weight_out.T,
    )
    zout = reduce_plane(nz, ny, acc.reshape(gs.shape))
    return place(own_count, base.reshape(1), reqs, zout)


def solution(mesh):
    in_specs = (
        P(("group", "ray"), None),
        P("group", "ray"),
        P(("group", "ray"), None, None),
        P(("group", "ray"), None),
        P(("group", "ray"), None),
        P(None, ("group", "ray")),
        P(),
        P(),
        P(),
    )
    out_specs = P(("group", "ray"), None)
    return jax.shard_map(
        per_device, mesh=mesh, in_specs=in_specs, out_specs=out_specs, check_vma=False
    )
```

time: 439 us -> 106 us (0.24)
  waiting for transfers between devices: 274 us -> 0 us
  Pallas kernels: 0 us -> 97.7 us
  local copies, waits for them, and re-layouts: 53.5 us -> 7.28 us
  blocking collectives: 43.9 us -> 0 us
  other arithmetic: 29.4 us -> 0.72 us
  matrix products: 19.6 us -> 0 us
  between operations: 14.3 us -> 0.05 us
    unnamed x3 -> x0, waiting for transfers between devices: 196 us -> none
    pallas_call x0 -> x4, Pallas kernels: none -> 97.7 us  [the longest x1 41 us: fetch(): pl.pallas_call(functools.partial(fetch_kernel, nz, ny), out_shape=(jax.Sh...]
    all_gather x1 -> x0, waiting for transfers between devices: 78.5 us -> none  [per_device(): group_set = lax.all_gather(holdings, 'ray', axis=0, tiled=True)]
    all_to_all x3 -> x0, blocking collectives: 43.9 us -> none  [the longest x1 17.2 us: per_device(): lax.all_to_all(requests, 'group', split_axis=0, concat_axis=0, tiled=True)]
    dot_general x6 -> x0, matrix products: 19.6 us -> none  [the longest x1 4.9 us: per_device(): jnp.einsum('tiv,tic->tvc', weights_tiles, grads_tiles, preferred_element_...]
    dot_general x1 -> x0, local copies, waits for them, and re-layouts: 11.8 us -> none  [per_device(): jnp.einsum('tiv,tic->tvc', weights_tiles, grads_tiles, preferred_element_...]
    scatter-add x2 -> x0, other arithmetic: 11.8 us -> none  [the longest x1 10.6 us: per_device(): jax.ops.segment_sum(outer.reshape(tiles_dev, row_width), slots, num_segme...]
    select_n x1 -> x0, local copies, waits for them, and re-layouts: 10.1 us -> none  [per_device(): jnp.take(group_set, slots, axis=0).reshape(tiles_dev, voxels, channels)]
  transfers between devices with their start and end apart: 2 -> 0, of which waited for: 2 -> 0; matrix products, arithmetic and copies ran while one was open for 1% -> 0% of each run, Pallas kernels for 0% -> 0%
where the time goes in v1:
time: 106 us
  Pallas kernels  97.7 us (92%)
  local copies, waits for them, and re-layouts  7.28 us (7%)
    pallas_call x1, Pallas kernels, fetch(): pl.pallas_call(functools.partial(fetch_kernel, nz, ny), out_shape=(jax.Sh...  41 us
    pallas_call x1, Pallas kernels, reduce_plane(): pl.pallas_call(functools.partial(reduce_kernel, nz, ny), out_shape=jax.Sh...  34.6 us
    pallas_call x1, Pallas kernels, compute(): pl.pallas_call(compute_kernel, out_shape=jax.ShapeDtypeStruct(gs.shape, F...  19.5 us
    unnamed x16, local copies, waits for them, and re-layouts  7.28 us
    pallas_call x1, Pallas kernels, place(): pl.pallas_call(place_kernel, out_shape=jax.ShapeDtypeStruct((own_count, 4...  2.54 us

profile of v1, /device:TPU:1, one launch (start us, length us, event | category | flops | bytes accessed | tf_op | source)
XLA Modules:
  0.0 105.7 jit_solution(11498882073285080081)
XLA Ops:
  0.0 0.7 fusion.7.slots_ref
  0.7 41.0 %fetch.1 = (bf16[2,4,8,2,32,128]{5,4,3,2,1,0:T(8,128)(2,1)}, s32[8,8,128]{2,1,0:T(8,128)}) custom-call(s32[1,2]{1,0:T(1,128)} %wb_ref.1, bf16[32,4096]{1,0:T(8,128)(2,1)} %bricks_ref.1), custom_call_target="tpu_custom_call" | custom-call | tf_op jit(solution)/shard_map/fetch/pallas_call | solution.py:172
  41.7 0.0 copy-start.1
  41.7 1.2 %copy-done.1 = bf16[2,4,8,2,32,128]{5,4,3,2,1,0:T(8,128)(2,1)S(1)} copy-done((bf16[2,4,8,2,32,128]{5,4,3,2,1,0:T(8,128)(2,1)S(1)}, bf16[2,4,8,2,32,128]{5,4,3,2,1,0:T(8,128)(2,1)}, u32[]{:S(2)}) %copy-start.1) | copy-done | bytes 1048600
  43.0 0.0 copy-start.2
  43.0 1.0 copy-done.2
  43.9 0.0 copy-start.3
  43.9 0.9 copy-done.3
  44.8 0.0 copy-start.4
  44.8 0.8 copy-done.4
  45.6 0.0 copy-start.5
  45.6 0.7 copy-done.5
  46.3 0.0 copy-start.6
  46.3 0.7 copy-done.6
  47.0 0.0 copy-start.7
  47.0 0.7 copy-done.7
  47.7 19.5 %compute.1 = f32[128,32,128]{2,1,0:T(8,128)S(1)} custom-call(s32[5,64]{1,0:T(8,128)S(1)} %fusion.7.slots_ref, bf16[5,64,512]{2,1,0:T(8,128)(2,1)S(1)} %bitcast.27, bf16[128,32,128]{2,1,0:T(8,128)(2,1)S(1)} %bitcast.26, f32[40,64]{1,0:T(8,128)S(1)} %bitcast.28, f32[3,64]{1,0:T(4,128)S(1)} %copy-done.6, bf16[64,256]{1,0:T(8,128)(2,1)S(1)} %copy-done.4, ...), custom_call_target="tpu_custom_call" | custom-call | tf_op jit(solution)/shard_map/compute/pallas_call | solution.py:457
  67.2 0.0 copy-start
  67.2 1.3 %copy-done = f32[128,32,128]{2,1,0:T(8,128)} copy-done((f32[128,32,128]{2,1,0:T(8,128)}, f32[128,32,128]{2,1,0:T(8,128)S(1)}, u32[]{:S(2)}) %copy-start) | copy-done | bytes 2097176
  68.5 34.6 %reduce_plane.1 = f32[8,2,32,128]{3,2,1,0:T(8,128)} custom-call(f32[2,4,8,2,32,128]{5,4,3,2,1,0:T(8,128)} %bitcast.25), custom_call_target="tpu_custom_call" | custom-call | tf_op jit(solution)/shard_map/reduce_plane/pallas_call | solution.py:261
  103.2 2.5 %place.1 = f32[32,4096]{1,0:T(8,128)} custom-call(s32[1]{0:T(128)} %bitcast.base_ref, s32[8,8,128]{2,1,0:T(8,128)} %get-tuple-element.7.reqs_ref, f32[512,128]{1,0:T(8,128)} %bitcast.30), custom_call_target="tpu_custom_call" | custom-call | tf_op jit(solution)/shard_map/place/pallas_call | solution.py:298
Async XLA Ops:
  41.7 1.2 %copy-start.1 = (bf16[2,4,8,2,32,128]{5,4,3,2,1,0:T(8,128)(2,1)S(1)}, bf16[2,4,8,2,32,128]{5,4,3,2,1,0:T(8,128)(2,1)}, u32[]{:S(2)}) copy-start(bf16[2,4,8,2,32,128]{5,4,3,2,1,0:T(8,128)(2,1)} %get-tuple-element.8) | copy-start | bytes 3145732
  43.0 1.0 copy-start.2
  43.9 0.9 copy-start.3
  44.8 0.8 copy-start.4
  45.6 0.7 copy-start.5
  46.3 0.7 copy-start.6
  47.0 0.7 copy-start.7
  67.2 1.3 %copy-start = (f32[128,32,128]{2,1,0:T(8,128)}, f32[128,32,128]{2,1,0:T(8,128)S(1)}, u32[]{:S(2)}) copy-start(f32[128,32,128]{2,1,0:T(8,128)S(1)} %compute.1) | copy-start | bytes 6291460

commit v2 on v1

v2 whole, which is shorter than its diff:
```python
import functools

import jax
import jax.numpy as jnp
from jax import lax
from jax.experimental import pallas as pl
from jax.experimental.pallas import tpu as pltpu
from jax.sharding import PartitionSpec as P

MESH = pl.DeviceIdType.MESH
F32 = jnp.float32
BF16 = jnp.bfloat16
NX = 4
NC = 2
PIECES = 1
PITCH = 40
HIGHEST = lax.Precision.HIGHEST


def coordinates():
    ray = lax.axis_index("ray")
    return ray // (NX * NC), (ray // NC) % NX, ray % NC


def ray_of(y, x, c):
    return (y * NX + x) * NC + c


class Peers:
    def __init__(self, nz, ny):
        self.nz, self.ny = nz, ny
        self.z = lax.axis_index("group")
        self.y, self.x, self.c = coordinates()

    def along_z(self, d):
        return {"group": lax.rem(self.z + d, self.nz)}

    def along_y(self, d):
        return {"ray": ray_of(lax.rem(self.y + d, self.ny), self.x, self.c)}

    def along_x(self, d):
        return {"ray": ray_of(self.y, lax.rem(self.x + d, NX), self.c)}

    def partner(self):
        return {"ray": ray_of(self.y, self.x, 1 - self.c)}

    def everybody(self):
        out = [self.along_z(d) for d in range(1, self.nz)]
        out += [self.along_y(d) for d in range(1, self.ny)]
        return out + [self.along_x(d) for d in range(1, NX)] + [self.partner()]

    def barrier(self):
        sem = pltpu.get_barrier_semaphore()
        peers = self.everybody()
        for peer in peers:
            pl.semaphore_signal(sem, inc=1, device_id=peer, device_id_type=MESH)
        pl.semaphore_wait(sem, len(peers))


class Copies:
    def __init__(self, send_sems, recv_sems):
        self.send_sems, self.recv_sems, self.count, self.live = send_sems, recv_sems, 0, []

    def make(self, src, dst, device):
        at = self.count
        self.count += 1
        copy = pltpu.make_async_remote_copy(
            src_ref=src,
            dst_ref=dst,
            send_sem=self.send_sems.at[at],
            recv_sem=self.recv_sems.at[at],
            device_id=device,
            device_id_type=MESH,
        )
        self.live.append(copy)
        return copy

    def start(self, src, dst, device):
        copy = self.make(src, dst, device)
        copy.start()
        return copy

    def drain(self):
        for copy in self.live:
            copy.wait_send()


def near_first(n):
    out = []
    for d in range(1, n // 2 + 1):
        out.append(d)
        if n - d != d:
            out.append(n - d)
    return out


def fetch_copies(nz, ny):
    return (nz - 1) + 2 * ((nz - 1) + (ny - 1)) + 3 * ny + 4 * ny


def fetch_kernel(
    nz,
    ny,
    wb_ref,
    slot_ref,
    bricks_hbm,
    gs_hbm,
    reqs_ref,
    place_ref,
    mine,
    bricks,
    picks,
    sendb,
    arrived,
    gs,
    load_sem,
    save_sem,
    send_sems,
    recv_sems,
):
    peers = Peers(nz, ny)
    copies = Copies(send_sems, recv_sems)
    load = pltpu.make_async_copy(bricks_hbm, bricks, load_sem.at[0])
    load.start()
    own_count = bricks.shape[0]
    row = lax.broadcasted_iota(jnp.int32, mine.shape, 0)
    tile = jnp.where(row == 0, wb_ref[0, 0], wb_ref[0, 1])
    mine[...] = tile
    reqs_ref[0] = tile
    peers.barrier()
    asks = [copies.start(mine, reqs_ref.at[nz - d], peers.along_z(d)) for d in near_first(nz)]
    slot = slot_ref[...]
    holder = slot // 2
    rel_y = lax.rem(holder // (NX * NC) + (ny - peers.y), ny)
    rel_x = lax.rem(lax.rem(holder // NC, NX) + (NX - peers.x), NX)
    rel_c = jnp.abs(lax.rem(holder, NC) - peers.c)
    place_ref[...] = ((rel_c * NX + rel_x) * ny + rel_y) * 2 + lax.rem(slot, 2)
    load.wait()
    for ask in asks:
        ask.wait_recv()
    base = (lax.axis_index("group") * lax.axis_size("ray") + lax.axis_index("ray")) * own_count
    lane = lax.broadcasted_iota(jnp.int32, (nz, 128), 1)
    rows = []
    for s in range(2):
        ids = jnp.concatenate([reqs_ref[e, s : s + 1, :] for e in range(nz)], axis=0)
        rows.append(jnp.where(ids - base == lane, 1.0, 0.0).astype(F32))
    choose = jnp.concatenate(rows, axis=0)[:, :own_count].astype(BF16)
    picked = jnp.dot(choose, bricks[...], preferred_element_type=F32)
    gives = {}
    for s in range(2):
        for p in range(32):
            picks[pl.ds(s * nz * PITCH + p, nz, stride=PITCH), :] = picked[
                s * nz : (s + 1) * nz, p * 128 : (p + 1) * 128
            ]
        rows = picks[s * nz * PITCH : (s + 1) * nz * PITCH, :].reshape(nz, PITCH, 128)
        sendb[s] = rows[:, :32].astype(BF16)
        for d in near_first(nz):
            gives[s, d] = copies.start(
                sendb.at[s, d], arrived.at[s, nz - d], peers.along_z(d)
            )
    right, far, left = (peers.along_x(d) for d in (1, 2, 3))
    partner = peers.partner()
    order = [0] + [ny - d for d in near_first(ny)]
    spread, hops, cores = {}, {}, []

    def to_core(j, e):
        cores.append(copies.start(gs.at[j, e], gs_hbm.at[1, j, e], partner))

    def along_row(e):
        for j, device in ((3, right), (1, left), (2, far)):
            hops[j, e] = copies.start(gs.at[0, e], gs.at[j, e], device)
        to_core(0, e)

    for s in range(2):
        held = sendb[s, 0].astype(F32)
        for d in near_first(nz):
            gives[s, d].wait_recv()
            held = held + arrived[s, nz - d].astype(F32)
        gs[0, 0, s] = held.astype(BF16)
        for d in near_first(ny):
            spread[s, ny - d] = copies.start(
                gs.at[0, 0, s], gs.at[0, ny - d, s], peers.along_y(d)
            )
    along_row(0)
    for e in order[1:]:
        spread[0, e].wait_recv()
        spread[1, e].wait_recv()
        along_row(e)
    for e in order:
        for j in (3, 1, 2):
            hops[j, e].wait_recv()
            to_core(j, e)
    save = pltpu.make_async_copy(gs, gs_hbm.at[0], save_sem.at[0])
    save.start()
    for copy in cores:
        copy.wait_recv()
    save.wait()
    copies.drain()


def fetch(nz, ny, work_bricks, slots, bricks):
    total = fetch_copies(nz, ny)
    vmem = pl.BlockSpec(memory_space=pltpu.VMEM)
    hbm = pl.BlockSpec(memory_space=pltpu.HBM)
    return pl.pallas_call(
        functools.partial(fetch_kernel, nz, ny),
        out_shape=(
            jax.ShapeDtypeStruct((NC, NX, ny, 2, 32, 128), BF16),
            jax.ShapeDtypeStruct((nz, 8, 128), jnp.int32),
            jax.ShapeDtypeStruct(slots.shape, jnp.int32),
        ),
        in_specs=[pl.BlockSpec(memory_space=pltpu.SMEM), vmem, hbm],
        out_specs=(hbm, vmem, vmem),
        scratch_shapes=[
            pltpu.VMEM((8, 128), jnp.int32),
            pltpu.VMEM(bricks.shape, BF16),
            pltpu.VMEM((2 * nz * PITCH, 128), F32),
            pltpu.VMEM((2, nz, 32, 128), BF16),
            pltpu.VMEM((2, nz, 32, 128), BF16),
            pltpu.VMEM((NX, ny, 2, 32, 128), BF16),
            pltpu.SemaphoreType.DMA((1,)),
            pltpu.SemaphoreType.DMA((1,)),
            pltpu.SemaphoreType.DMA((total,)),
            pltpu.SemaphoreType.DMA((total,)),
        ],
        compiler_params=pltpu.CompilerParams(collective_id=0, has_side_effects=True),
        name="fetch",
    )(work_bricks, slots, bricks)


def reduce_kernel(
    nz,
    ny,
    acc_hbm,
    zout_ref,
    cbuf,
    part,
    relay_a,
    relay_b,
    from_left,
    from_right,
    ybuf,
    load_sems,
    send_sems,
    recv_sems,
):
    peers = Peers(nz, ny)
    copies = Copies(send_sems, recv_sems)
    slices = acc_hbm.shape[0]
    used = pl.ds(0, acc_hbm.shape[-2])
    half = ny // 2
    a, b = pl.ds(0, half), pl.ds(half, half)
    right, left, partner = peers.along_x(1), peers.along_x(NX - 1), peers.partner()
    loads = []
    for q in range(slices):
        load = pltpu.make_async_copy(acc_hbm.at[q, 0], part.at[q], load_sems.at[q])
        load.start()
        loads.append(load)
    peers.barrier()
    core, far_a, far_b, left_a, left_b, right_a, right_b = {}, {}, {}, {}, {}, {}, {}
    for q in range(slices):
        for j in (2, 1, 3, 0):
            core[q, j] = copies.start(acc_hbm.at[q, 1, j], cbuf.at[q, j], partner)

    def merge(q, j):
        core[q, j].wait_recv()
        part[q, j] = part[q, j] + cbuf[q, j]

    for q in range(slices):
        loads[q].wait()
        merge(q, 2)
        far_a[q] = copies.start(part.at[q, 2, a], relay_a.at[q], right)
        far_b[q] = copies.start(part.at[q, 2, b], relay_b.at[q], left)
        merge(q, 1)
        left_b[q] = copies.start(part.at[q, 1, b], from_left.at[q, b], right)
        merge(q, 3)
        right_a[q] = copies.start(part.at[q, 3, a], from_right.at[q, a], left)
    for q in range(slices):
        far_a[q].wait_recv()
        part[q, 1, a] = part[q, 1, a] + relay_a[q]
        left_a[q] = copies.start(part.at[q, 1, a], from_left.at[q, a], right)
        far_b[q].wait_recv()
        part[q, 3, b] = part[q, 3, b] + relay_b[q]
        right_b[q] = copies.start(part.at[q, 3, b], from_right.at[q, b], left)
        merge(q, 0)
    ys, zs = {}, []
    for q in range(slices):
        for copy, side in ((right_a, a), (left_a, a), (left_b, b), (right_b, b)):
            copy[q].wait_recv()
        part[q, 0] = part[q, 0] + from_left[q] + from_right[q]
        for d in near_first(ny):
            ys[q, d] = copies.start(part.at[q, 0, d], ybuf.at[q, ny - d], peers.along_y(d))
    for q in range(slices):
        mine = part[q, 0, 0]
        for d in near_first(ny):
            ys[q, d].wait_recv()
            mine = mine + ybuf[q, ny - d]
        zout_ref[q, 0, used] = mine
        for d in near_first(nz):
            zs.append(
                copies.start(
                    zout_ref.at[q, 0, used], zout_ref.at[q, nz - d, used], peers.along_z(d)
                )
            )
    for copy in zs:
        copy.wait_recv()
    copies.drain()


def reduce_plane(nz, ny, acc):
    slices, unit = acc.shape[0], acc.shape[-2:]
    total = slices * (4 + 6 + (ny - 1) + (nz - 1))
    vmem = pl.BlockSpec(memory_space=pltpu.VMEM)
    half = (slices, ny // 2) + unit
    whole = (slices, ny) + unit
    every = (slices, NX, ny) + unit
    return pl.pallas_call(
        functools.partial(reduce_kernel, nz, ny),
        out_shape=jax.ShapeDtypeStruct((slices, nz, unit[0] + 8, 128), F32),
        in_specs=[pl.BlockSpec(memory_space=pltpu.HBM)],
        out_specs=vmem,
        scratch_shapes=[
            pltpu.VMEM(every, F32),
            pltpu.VMEM(every, F32),
            pltpu.VMEM(half, F32),
            pltpu.VMEM(half, F32),
            pltpu.VMEM(whole, F32),
            pltpu.VMEM(whole, F32),
            pltpu.VMEM(whole, F32),
            pltpu.SemaphoreType.DMA((slices,)),
            pltpu.SemaphoreType.DMA((total,)),
            pltpu.SemaphoreType.DMA((total,)),
        ],
        compiler_params=pltpu.CompilerParams(collective_id=1, has_side_effects=True),
        name="reduce_plane",
    )(acc)


def place_kernel(unit, base_ref, reqs_ref, z_ref, out_ref):
    nz = reqs_ref.shape[0]
    own_count = out_ref.shape[0]
    lane = lax.broadcasted_iota(jnp.int32, (2 * nz, 128), 1)
    ids = [reqs_ref[e, s : s + 1, :] for s in range(2) for e in range(nz)]
    hit = jnp.where(jnp.concatenate(ids, axis=0) - base_ref[0] == lane, 1.0, 0.0).astype(F32)
    spread = jnp.transpose(hit)[:own_count]
    for p in range(32):
        at = p // unit * (2 * nz * (unit + 8)) + p % unit
        rows = z_ref[pl.ds(at, 2 * nz, stride=unit + 8), :]
        out_ref[:, p * 128 : (p + 1) * 128] = jnp.dot(
            spread, rows, precision=HIGHEST, preferred_element_type=F32
        )


def place(own_count, base, reqs, zout):
    vmem = pl.BlockSpec(memory_space=pltpu.VMEM)
    return pl.pallas_call(
        functools.partial(place_kernel, zout.shape[-2] - 8),
        out_shape=jax.ShapeDtypeStruct((own_count, 4096), F32),
        in_specs=[pl.BlockSpec(memory_space=pltpu.SMEM), vmem, vmem],
        out_specs=vmem,
        name="place",
    )(base, reqs, zout.reshape(-1, 128))


def logistic(x):
    return 0.5 * jnp.tanh(0.5 * x) + 0.5


def silu_of_half(half):
    t = jnp.tanh(half)
    up = 1.0 + t
    act = half * up
    return act, up + act * (1.0 - t)


def compute_kernel(
    slots_ref,
    interp_hbm,
    gs_hbm,
    win_hbm,
    wmid_hbm,
    wout_hbm,
    spacing_hbm,
    targets_hbm,
    acc_hbm,
    interp_ref,
    gs_ref,
    win_ref,
    wmid_ref,
    wout_ref,
    spacing_ref,
    targets_ref,
    acc_ref,
    load_sems,
    wc,
    feat_a,
    feat_b,
    slope_a,
    slope_b,
    raw_s,
    grad_s,
    gfeat,
):
    segs, rays, _ = interp_ref.shape
    chunk = rays * 8
    steps = segs * 8
    pitch = rays + 8
    unroll = 16
    pieces_of, unit = acc_ref.shape[0], acc_ref.shape[2]
    loads = []
    for n, (src, dst) in enumerate(
        (
            (interp_hbm, interp_ref),
            (gs_hbm, gs_ref),
            (win_hbm, win_ref),
            (wmid_hbm, wmid_ref),
            (wout_hbm, wout_ref),
            (spacing_hbm, spacing_ref),
            (targets_hbm, targets_ref),
        )
    ):
        loads.append(pltpu.make_async_copy(src, dst, load_sems.at[n]))
        loads[n].start()
    acc_ref[...] = jnp.zeros_like(acc_ref)
    loads[0].wait()

    src = lax.broadcasted_iota(jnp.int32, (128, 512), 0)
    dst = lax.broadcasted_iota(jnp.int32, (128, 512), 1)
    voxel = src % 64
    perm = jnp.where(
        (dst // 128 == (src // 64) * 2 + voxel % 2) & (dst % 128 == voxel // 2), 1.0, 0.0
    ).astype(BF16)
    for seg in range(segs):
        for j in range(4):
            moved = jnp.dot(
                interp_ref[seg, :, j * 128 : (j + 1) * 128], perm, preferred_element_type=F32
            )
            for i2 in range(2):
                for h in range(2):
                    blk = i2 * 2 + h
                    wc[pl.ds(seg * rays * 24 + h * 8 + 2 * j + i2, rays, stride=24), :] = moved[
                        :, blk * 128 : (blk + 1) * 128
                    ]
    for load in loads[1:]:
        load.wait()

    def tile_weights(tile):
        return wc[pl.ds(pl.multiple_of(tile * 24, 8), 16), :][:, :32].astype(BF16)

    win = win_ref[...] * 0.5
    wmid = wmid_ref[...] * 0.5
    wout = jnp.concatenate([wout_ref[...].astype(F32), jnp.zeros((4, 256), F32)], axis=0).astype(BF16)
    win_wide = jnp.concatenate([win.astype(F32), jnp.zeros((64, 256), F32)], axis=0).astype(BF16)

    for seg in range(segs):

        @pl.loop(0, rays // unroll)
        def _(group):
            for u in range(unroll):
                r = group * unroll + u
                brick = gs_ref[slots_ref[seg, r]]
                made = jnp.dot(tile_weights(seg * rays + r), brick, preferred_element_type=F32)
                feat_a[pl.ds(r, 8, stride=pitch), :] = made[:8]
                feat_b[pl.ds(r, 8, stride=pitch), :] = made[8:]

        rows = pl.ds(seg * chunk, chunk)
        features = (feat_a[...] + pltpu.roll(feat_b[...], 64, 1)).reshape(8, pitch, 128)
        features = features[:, :rays].reshape(chunk, 128)[:, :64].astype(BF16)
        act, slope_a[rows, :] = silu_of_half(jnp.dot(features, win, preferred_element_type=F32))
        act, slope_b[rows, :] = silu_of_half(
            jnp.dot(act.astype(BF16), wmid, preferred_element_type=F32)
        )
        raw = lax.dot_general(
            wout, act.astype(BF16), (((1,), (1,)), ((), ())), preferred_element_type=F32
        )
        turned = pltpu.roll(raw, chunk - rays, 1)
        for i in range(0, 8, 2):
            at = i * rays
            raw_s[pl.ds(seg * 8 + i, 8, stride=steps), :] = raw[:, at : at + 128]
            raw_s[pl.ds(seg * 8 + i + 1, 8, stride=steps), :] = turned[:, at : at + 128]

    spacing = spacing_ref[...]
    k0 = lax.broadcasted_iota(jnp.int32, (steps, steps), 0)
    k1 = lax.broadcasted_iota(jnp.int32, (steps, steps), 1)
    earlier = jnp.where(k1 < k0, 1.0, 0.0).astype(F32)
    later = jnp.where(k1 > k0, 1.0, 0.0).astype(F32)
    raw0 = raw_s[0:steps, :][:, :rays]
    density = jnp.maximum(raw0, 0.0) + jnp.log1p(jnp.exp(-jnp.abs(raw0)))
    optical = density * spacing
    before = jnp.dot(earlier, optical, precision=HIGHEST, preferred_element_type=F32)
    through = jnp.exp(-before)
    kept = jnp.exp(-optical)
    weight = through * (1.0 - kept)
    pull = jnp.zeros_like(weight)
    grads = []
    for ch in range(3):
        shade = logistic(raw_s[(ch + 1) * steps : (ch + 2) * steps, :][:, :rays])
        colour = jnp.sum(weight * shade, axis=0, keepdims=True)
        err = colour - targets_ref[ch : ch + 1, :]
        pull = pull + err * shade
        grads.append(err * weight * shade * (1.0 - shade))
    after = jnp.dot(later, pull * weight, precision=HIGHEST, preferred_element_type=F32)
    grads.insert(0, (pull * through * kept - after) * spacing * logistic(raw0))
    grad_s[...] = jnp.zeros_like(grad_s)
    for ch in range(4):
        grad_s[ch * steps : (ch + 1) * steps, :rays] = grads[ch]

    for seg in range(segs):
        pieces = []
        for i in range(0, 8, 2):
            even = grad_s[pl.ds(seg * 8 + i, 8, stride=steps), :]
            odd = grad_s[pl.ds(seg * 8 + i + 1, 8, stride=steps), :]
            pieces.append(even + pltpu.roll(odd, rays, 1))
        raw_grad = jnp.concatenate(pieces, axis=1).astype(BF16)
        rows = pl.ds(seg * chunk, chunk)
        grad = lax.dot_general(
            raw_grad, wout, (((0,), (0,)), ((), ())), preferred_element_type=F32
        )
        slope = (grad * slope_b[rows, :]).astype(BF16)
        grad = lax.dot_general(slope, wmid, (((1,), (1,)), ((), ())), preferred_element_type=F32)
        slope = (grad * slope_a[rows, :]).astype(BF16)
        grad = lax.dot_general(
            slope, win_wide, (((1,), (1,)), ((), ())), preferred_element_type=F32
        )
        grad = grad.astype(BF16).astype(F32)
        for i in range(8):
            gfeat[i * pitch : i * pitch + rays, :] = grad[i * rays : (i + 1) * rays]

        @pl.loop(0, rays // unroll)
        def _(group):
            for u in range(unroll):
                r = group * unroll + u
                g = gfeat[pl.ds(r, 8, stride=pitch), :]
                both = jnp.concatenate([g, pltpu.roll(g, 64, 1)], axis=0).astype(BF16)
                outer = lax.dot_general(
                    tile_weights(seg * rays + r),
                    both,
                    (((0,), (0,)), ((), ())),
                    preferred_element_type=F32,
                )
                slot = slots_ref[seg, r]
                slot = (slot & 1) * (acc_ref.shape[1] // 2) + (slot >> 1)
                for n in range(pieces_of):
                    acc_ref[n, slot] = acc_ref[n, slot] + outer[n * unit : (n + 1) * unit]

    save = pltpu.make_async_copy(acc_ref, acc_hbm, load_sems.at[0])
    save.start()
    save.wait()


def compute(slots, interp, gs, weight_in, weight_mid, weight_out, spacing, targets):
    segs, rays, _ = interp.shape
    tiles, samples = segs * rays, segs * rays * 8
    hbm = pl.BlockSpec(memory_space=pltpu.HBM)
    operands = (interp, gs, weight_in, weight_mid, weight_out, spacing, targets)
    acc = jax.ShapeDtypeStruct((PIECES, gs.shape[0], 32 // PIECES, 128), F32)
    return pl.pallas_call(
        compute_kernel,
        out_shape=acc,
        in_specs=[pl.BlockSpec(memory_space=pltpu.SMEM)] + [hbm] * 7,
        out_specs=hbm,
        scratch_shapes=[pltpu.VMEM(x.shape, x.dtype) for x in operands]
        + [
            pltpu.VMEM(acc.shape, F32),
            pltpu.SemaphoreType.DMA((7,)),
            pltpu.VMEM((tiles * 24, 128), F32),
            pltpu.VMEM(((rays + 8) * 8, 128), F32),
            pltpu.VMEM(((rays + 8) * 8, 128), F32),
            pltpu.VMEM((samples, 256), F32),
            pltpu.VMEM((samples, 256), F32),
            pltpu.VMEM((8 * segs * 8, 128), F32),
            pltpu.VMEM((8 * segs * 8, 128), F32),
            pltpu.VMEM(((rays + 8) * 8, 128), F32),
        ],
        name="compute",
    )(slots, *operands)


def per_device(
    bricks, work_bricks, interp, tile_slot, spacing, targets, weight_in, weight_mid, weight_out
):
    nz = lax.axis_size("group")
    ny = lax.axis_size("ray") // (NX * NC)
    own_count = bricks.shape[0]
    base = (lax.axis_index("group") * lax.axis_size("ray") + lax.axis_index("ray")) * own_count
    gs, reqs, slots = fetch(nz, ny, work_bricks, tile_slot.T, bricks)
    acc = compute(
        slots,
        interp.transpose(1, 0, 2),
        gs.reshape(-1, 32, 128),
        weight_in,
        weight_mid,
        weight_out.T,
        spacing.T,
        targets,
    )
    zout = reduce_plane(nz, ny, acc.reshape((2 * PIECES, NC, NX, ny) + acc.shape[2:]))
    return place(own_count, base.reshape(1), reqs, zout)


def solution(mesh):
    in_specs = (
        P(("group", "ray"), None),
        P("group", "ray"),
        P(("group", "ray"), None, None),
        P(("group", "ray"), None),
        P(("group", "ray"), None),
        P(None, ("group", "ray")),
        P(),
        P(),
        P(),
    )
    out_specs = P(("group", "ray"), None)
    return jax.shard_map(
        per_device, mesh=mesh, in_specs=in_specs, out_specs=out_specs, check_vma=False
    )
```

time: 106 us -> 91.6 us (0.86)
  local copies, waits for them, and re-layouts: 7.28 us -> 0 us
  Pallas kernels: 97.7 us -> 91.2 us
    unnamed x16 -> x0, local copies, waits for them, and re-layouts: 7.28 us -> none
    pallas_call x1, Pallas kernels: 34.6 us -> 30.1 us  [reduce_plane(): pl.pallas_call(functools.partial(reduce_kernel, nz, ny), out_shape=jax.Sh...]
    pallas_call x1, Pallas kernels: 41 us -> 38.6 us  [fetch(): pl.pallas_call(functools.partial(fetch_kernel, nz, ny), out_shape=(jax.Sh...]
where the time goes in v2:
time: 91.6 us; the launch traced here: 91.2 us
  Pallas kernels  91.2 us (100%)
    pallas_call x1, Pallas kernels, fetch(): pl.pallas_call(functools.partial(fetch_kernel, nz, ny), out_shape=(jax.Sh...  38.6 us
    pallas_call x1, Pallas kernels, reduce_plane(): pl.pallas_call(functools.partial(reduce_kernel, nz, ny), out_shape=jax.Sh...  30.1 us
    pallas_call x1, Pallas kernels, compute(): pl.pallas_call(compute_kernel, out_shape=acc, in_specs=[pl.BlockSpec(memo...  19.9 us
    pallas_call x1, Pallas kernels, place(): pl.pallas_call(functools.partial(place_kernel, zout.shape[-2] - 8), out_s...  2.57 us

profile of v2, /device:TPU:1, one launch (start us, length us, event | category | flops | bytes accessed | tf_op | source)
XLA Modules:
  0.0 91.2 jit_solution(17458718957398392432)
XLA Ops:
  0.0 38.6 %fetch.1 = (bf16[2,4,8,2,32,128]{5,4,3,2,1,0:T(8,128)(2,1)}, s32[8,8,128]{2,1,0:T(8,128)}, s32[5,64]{1,0:T(8,128)}) custom-call(s32[1,2]{1,0:T(1,128)} %wb_ref.1, s32[5,64]{1,0:T(8,128)} %bitcast.13, bf16[32,4096]{1,0:T(8,128)(2,1)} %bricks_hbm.1), custom_call_target="tpu_custom_call" | custom-call | tf_op jit(solution)/shard_map/fetch/pallas_call | solution.py:205
  38.6 19.9 %compute.1 = f32[1,128,32,128]{3,2,1,0:T(8,128)} custom-call(s32[5,64]{1,0:T(8,128)} %get-tuple-element.9.slots_ref, bf16[5,64,512]{2,1,0:T(8,128)(2,1)} %bitcast.11, bf16[128,32,128]{2,1,0:T(8,128)(2,1)} %bitcast.10, bf16[64,256]{1,0:T(8,128)(2,1)} %win_hbm.1, bf16[256,256]{1,0:T(8,128)(2,1)} %wmid_hbm.1, bf16[4,256]{1,0:T(4,128)(2,1)} %bitcast.14, ...), custom_call_target="tpu_custom_call" | custom-call | tf_op jit(solution)/shard_map/compute/pallas_call | solution.py:557
  58.5 30.1 %reduce_plane.1 = f32[2,8,40,128]{3,2,1,0:T(8,128)} custom-call(f32[2,2,4,8,32,128]{5,4,3,2,1,0:T(8,128)} %bitcast.8), custom_call_target="tpu_custom_call" | custom-call | tf_op jit(solution)/shard_map/reduce_plane/pallas_call | solution.py:317
  88.6 2.6 %place.1 = f32[32,4096]{1,0:T(8,128)} custom-call(s32[1]{0:T(128)} %bitcast.base_ref, s32[8,8,128]{2,1,0:T(8,128)} %get-tuple-element.8.reqs_ref, f32[640,128]{1,0:T(8,128)} %bitcast.9), custom_call_target="tpu_custom_call" | custom-call | tf_op jit(solution)/shard_map/place/pallas_call | solution.py:356

commit v3 on v0

v3 whole, which is shorter than its diff:
```python
import functools

import jax
import jax.numpy as jnp
from jax import lax
from jax.experimental import pallas as pl
from jax.experimental.pallas import tpu as pltpu
from jax.sharding import PartitionSpec as P

MESH = pl.DeviceIdType.MESH
F32 = jnp.float32
BF16 = jnp.bfloat16
NX = 4
NC = 2
PITCH = 40
HIGHEST = lax.Precision.HIGHEST


def coordinates():
    ray = lax.axis_index("ray")
    return ray // (NX * NC), (ray // NC) % NX, ray % NC


def ray_of(y, x, c):
    return (y * NX + x) * NC + c


class Peers:
    def __init__(self, nz, ny):
        self.nz, self.ny = nz, ny
        self.z = lax.axis_index("group")
        self.y, self.x, self.c = coordinates()

    def along_z(self, d):
        return {"group": lax.rem(self.z + d, self.nz)}

    def along_y(self, d):
        return {"ray": ray_of(lax.rem(self.y + d, self.ny), self.x, self.c)}

    def along_x(self, d):
        return {"ray": ray_of(self.y, lax.rem(self.x + d, NX), self.c)}

    def partner(self):
        return {"ray": ray_of(self.y, self.x, 1 - self.c)}

    def everybody(self):
        out = [self.along_z(d) for d in range(1, self.nz)]
        out += [self.along_y(d) for d in range(1, self.ny)]
        return out + [self.along_x(d) for d in range(1, NX)] + [self.partner()]

    def greet(self):
        sem = pltpu.get_barrier_semaphore()
        peers = self.everybody()
        for peer in peers:
            pl.semaphore_signal(sem, inc=1, device_id=peer, device_id_type=MESH)
        return lambda: pl.semaphore_wait(sem, len(peers))


class Copies:
    def __init__(self, send_sems, recv_sems):
        self.send_sems, self.recv_sems, self.count, self.live = send_sems, recv_sems, 0, []

    def make(self, src, dst, device):
        at = self.count
        self.count += 1
        copy = pltpu.make_async_remote_copy(
            src_ref=src,
            dst_ref=dst,
            send_sem=self.send_sems.at[at],
            recv_sem=self.recv_sems.at[at],
            device_id=device,
            device_id_type=MESH,
        )
        self.live.append(copy)
        return copy

    def start(self, src, dst, device):
        copy = self.make(src, dst, device)
        copy.start()
        return copy

    def drain(self):
        for copy in self.live:
            copy.wait_send()


def near_first(n):
    out = []
    for d in range(1, n // 2 + 1):
        out.append(d)
        if n - d != d:
            out.append(n - d)
    return out


def logistic(x):
    return 0.5 * jnp.tanh(0.5 * x) + 0.5


def silu_of_half(half):
    t = jnp.tanh(half)
    up = 1.0 + t
    act = half * up
    return act, up + act * (1.0 - t)


def iota(shape, axis):
    return lax.broadcasted_iota(jnp.int32, shape, axis)


def indicator(condition, dtype=F32):
    return jnp.where(condition, 1.0, 0.0).astype(dtype)


def step_copies(nz, ny):
    fetched = 2 * (nz - 1) + (nz - 1) + 2 * (ny - 1) + 3 * ny + 4 * ny
    return fetched + 2 * (4 + 6 + (ny - 1) + (nz - 1))


def step_kernel(
    nz,
    ny,
    wb_ref,
    slots_ref,
    slotv_ref,
    bricks_hbm,
    interp_hbm,
    win_hbm,
    wmid_hbm,
    wout_hbm,
    spacing_hbm,
    targets_hbm,
    zout_ref,
    reqs_ref,
    bricks_ref,
    interp_ref,
    win_ref,
    wmid_ref,
    wout_ref,
    spacing_ref,
    targets_ref,
    mine,
    picks,
    sendb,
    arrived,
    gs,
    wc,
    feat_a,
    feat_b,
    slope_a,
    slope_b,
    raw_s,
    grad_s,
    order_s,
    parity_s,
    wsort,
    wturned,
    gnat,
    gsort,
    outb,
    part,
    cbuf,
    relay_a,
    relay_b,
    from_left,
    from_right,
    ybuf,
    load_sems,
    send_sems,
    recv_sems,
):
    peers = Peers(nz, ny)
    copies = Copies(send_sems, recv_sems)
    segs, rays, _ = interp_ref.shape
    tiles = segs * rays
    holders = NC * NX * ny
    cap = 2 * tiles // holders
    sorted_rows = holders * cap
    chunk = rays * 8
    steps = segs * 8
    pitch = rays + 8
    own_count = bricks_ref.shape[0]
    loads = []
    for n, (src, dst) in enumerate(
        (
            (interp_hbm, interp_ref),
            (bricks_hbm, bricks_ref),
            (win_hbm, win_ref),
            (wmid_hbm, wmid_ref),
            (wout_hbm, wout_ref),
            (spacing_hbm, spacing_ref),
            (targets_hbm, targets_ref),
        )
    ):
        loads.append(pltpu.make_async_copy(src, dst, load_sems.at[n]))
        loads[n].start()
    ask = jnp.where(iota(mine.shape, 0) == 0, wb_ref[0, 0], wb_ref[0, 1])
    mine[...] = ask
    reqs_ref[0] = ask
    barrier = peers.greet()

    slot = slotv_ref[...]
    holder = slot // 2
    rel_y = lax.rem(holder // (NX * NC) + (ny - peers.y), ny)
    rel_x = lax.rem(lax.rem(holder // NC, NX) + (NX - peers.x), NX)
    rel_c = jnp.abs(lax.rem(holder, NC) - peers.c)
    rel = ((rel_c * NX + rel_x) * ny + rel_y).astype(F32)
    parity = lax.rem(slot, 2).astype(F32)

    def as_row(x):
        return jnp.concatenate([x[seg : seg + 1] for seg in range(segs)], axis=1)

    rel, parity = as_row(rel), as_row(parity)
    named = rel == iota((holders, tiles), 0).astype(F32)
    before = indicator(iota((tiles, tiles), 0) < iota((tiles, tiles), 1), BF16)
    counts = jnp.dot(indicator(named, BF16), before, preferred_element_type=F32)
    rank = jnp.sum(jnp.where(named, counts, 0.0), axis=0, keepdims=True)
    taken = rel * cap + rank
    order_s[...] = indicator(iota((sorted_rows, tiles), 0).astype(F32) == taken, BF16)

    src, dst = iota((128, 512), 0), iota((128, 512), 1)
    voxel = src % 64
    perm = indicator(
        (dst // 128 == (src // 64) * 2 + voxel % 2) & (dst % 128 == voxel // 2), BF16
    )
    loads[0].wait()
    for seg in range(segs):
        for j in range(4):
            moved = jnp.dot(
                interp_ref[seg, :, j * 128 : (j + 1) * 128], perm, preferred_element_type=F32
            )
            for i2 in range(2):
                for h in range(2):
                    blk = i2 * 2 + h
                    wc[pl.ds(seg * rays * 24 + h * 8 + 2 * j + i2, rays, stride=24), :] = moved[
                        :, blk * 128 : (blk + 1) * 128
                    ]
    barrier()
    asks = [copies.start(mine, reqs_ref.at[nz - d], peers.along_z(d)) for d in near_first(nz)]

    natural = interp_ref[...].reshape(tiles, 512)
    ordered = jnp.dot(order_s[...], natural, preferred_element_type=F32)
    for j in range(4):
        pair = ordered[:, j * 128 : (j + 1) * 128]
        wsort[pl.ds(2 * j, sorted_rows, stride=8), :] = pair
        wsort[pl.ds(2 * j + 1, sorted_rows, stride=8), :] = pltpu.roll(pair, 64, 1)
    lane128 = iota((sorted_rows, 128), 1)
    wide = jnp.broadcast_to(parity, (128, tiles)).astype(BF16)
    odd = lax.dot_general(
        order_s[...], wide, (((1,), (1,)), ((), ())), preferred_element_type=F32
    )
    parity_s[...] = indicator((lane128 >= 64) == (odd > 0.5))

    def turn(first, last):
        for h in range(first, last):
            block = wsort[h * cap * 8 : (h + 1) * cap * 8, :]
            wturned[h] = jnp.transpose(block)[:64].astype(BF16)

    for load in loads[1:]:
        load.wait()
    for copy in asks:
        copy.wait_recv()
    base = (lax.axis_index("group") * lax.axis_size("ray") + lax.axis_index("ray")) * own_count
    rows = []
    for s in range(2):
        ids = jnp.concatenate([reqs_ref[e, s : s + 1, :] for e in range(nz)], axis=0)
        rows.append(indicator(ids - base == iota((nz, 128), 1)))
    choose = jnp.concatenate(rows, axis=0)[:, :own_count].astype(BF16)
    picked = jnp.dot(choose, bricks_ref[...], preferred_element_type=F32)
    gives = {}
    for s in range(2):
        for p in range(32):
            picks[pl.ds(s * nz * PITCH + p, nz, stride=PITCH), :] = picked[
                s * nz : (s + 1) * nz, p * 128 : (p + 1) * 128
            ]
        rows = picks[s * nz * PITCH : (s + 1) * nz * PITCH, :].reshape(nz, PITCH, 128)
        sendb[s] = rows[:, :32].astype(BF16)
        for d in near_first(nz):
            gives[s, d] = copies.start(sendb.at[s, d], arrived.at[s, nz - d], peers.along_z(d))
    turn(0, holders // 2)
    right, far, left = (peers.along_x(d) for d in (1, 2, 3))
    partner = peers.partner()
    order = [0] + [ny - d for d in near_first(ny)]
    spread, hops, cores = {}, {}, []

    def unit(c, j, e):
        y = lax.rem(peers.y + e, ny)
        x = lax.rem(peers.x + j, NX)
        return ray_of(y, x, c)

    def to_core(j, e):
        at = unit(peers.c, j, e)
        cores.append(copies.start(gs.at[at], gs.at[at], partner))

    def along_row(e):
        at = unit(peers.c, 0, e)
        for j, device in ((3, right), (1, left), (2, far)):
            hops[j, e] = copies.start(gs.at[at], gs.at[at], device)
        to_core(0, e)

    for s in range(2):
        held = sendb[s, 0].astype(F32)
        for d in near_first(nz):
            gives[s, d].wait_recv()
            held = held + arrived[s, nz - d].astype(F32)
        at = unit(peers.c, 0, 0)
        gs[at, s] = held.astype(BF16)
        for d in near_first(ny):
            spread[s, ny - d] = copies.start(gs.at[at, s], gs.at[at, s], peers.along_y(d))
    along_row(0)
    turn(holders // 2, holders)
    for e in order[1:]:
        spread[0, e].wait_recv()
        spread[1, e].wait_recv()
        along_row(e)
    for e in order:
        for j in (3, 1, 2):
            hops[j, e].wait_recv()
            to_core(j, e)
    for copy in cores:
        copy.wait_recv()

    win = win_ref[...] * 0.5
    wmid = wmid_ref[...] * 0.5
    wout = jnp.concatenate([wout_ref[...].astype(F32), jnp.zeros((4, 256), F32)], axis=0).astype(BF16)
    win_wide = jnp.concatenate([win.astype(F32), jnp.zeros((64, 256), F32)], axis=0).astype(BF16)
    unroll = 16
    for seg in range(segs):

        @pl.loop(0, rays // unroll)
        def _(group):
            for u in range(unroll):
                r = group * unroll + u
                name = slots_ref[seg, r]
                brick = gs[name >> 1, name & 1]
                at = pl.multiple_of((seg * rays + r) * 24, 8)
                weights = wc[pl.ds(at, 16), :][:, :32].astype(BF16)
                made = jnp.dot(weights, brick, preferred_element_type=F32)
                feat_a[pl.ds(r, 8, stride=pitch), :] = made[:8]
                feat_b[pl.ds(r, 8, stride=pitch), :] = made[8:]

        rows = pl.ds(seg * chunk, chunk)
        features = (feat_a[...] + pltpu.roll(feat_b[...], 64, 1)).reshape(8, pitch, 128)
        features = features[:, :rays].reshape(chunk, 128)[:, :64].astype(BF16)
        act, slope_a[rows, :] = silu_of_half(jnp.dot(features, win, preferred_element_type=F32))
        act, slope_b[rows, :] = silu_of_half(
            jnp.dot(act.astype(BF16), wmid, preferred_element_type=F32)
        )
        raw = lax.dot_general(
            wout, act.astype(BF16), (((1,), (1,)), ((), ())), preferred_element_type=F32
        )
        turned = pltpu.roll(raw, chunk - rays, 1)
        for i in range(0, 8, 2):
            at = i * rays
            raw_s[pl.ds(seg * 8 + i, 8, stride=steps), :] = raw[:, at : at + 128]
            raw_s[pl.ds(seg * 8 + i + 1, 8, stride=steps), :] = turned[:, at : at + 128]

    spacing = spacing_ref[...]
    k0, k1 = iota((steps, steps), 0), iota((steps, steps), 1)
    earlier, later = indicator(k1 < k0), indicator(k1 > k0)
    raw0 = raw_s[0:steps, :][:, :rays]
    density = jnp.maximum(raw0, 0.0) + jnp.log1p(jnp.exp(-jnp.abs(raw0)))
    optical = density * spacing
    gone = jnp.dot(earlier, optical, precision=HIGHEST, preferred_element_type=F32)
    through = jnp.exp(-gone)
    kept = jnp.exp(-optical)
    weight = through * (1.0 - kept)
    pull = jnp.zeros_like(weight)
    grads = []
    for ch in range(3):
        shade = logistic(raw_s[(ch + 1) * steps : (ch + 2) * steps, :][:, :rays])
        colour = jnp.sum(weight * shade, axis=0, keepdims=True)
        err = colour - targets_ref[ch : ch + 1, :]
        pull = pull + err * shade
        grads.append(err * weight * shade * (1.0 - shade))
    after = jnp.dot(later, pull * weight, precision=HIGHEST, preferred_element_type=F32)
    grads.insert(0, (pull * through * kept - after) * spacing * logistic(raw0))
    grad_s[...] = jnp.zeros_like(grad_s)
    for ch in range(4):
        grad_s[ch * steps : (ch + 1) * steps, :rays] = grads[ch]

    for seg in range(segs):
        pieces = []
        for i in range(0, 8, 2):
            even = grad_s[pl.ds(seg * 8 + i, 8, stride=steps), :]
            uneven = grad_s[pl.ds(seg * 8 + i + 1, 8, stride=steps), :]
            pieces.append(even + pltpu.roll(uneven, rays, 1))
        raw_grad = jnp.concatenate(pieces, axis=1).astype(BF16)
        rows = pl.ds(seg * chunk, chunk)
        grad = lax.dot_general(
            raw_grad, wout, (((0,), (0,)), ((), ())), preferred_element_type=F32
        )
        slope = (grad * slope_b[rows, :]).astype(BF16)
        grad = lax.dot_general(slope, wmid, (((1,), (1,)), ((), ())), preferred_element_type=F32)
        slope = (grad * slope_a[rows, :]).astype(BF16)
        grad = lax.dot_general(
            slope, win_wide, (((1,), (1,)), ((), ())), preferred_element_type=F32
        )
        for j in range(4):
            even = grad[2 * j * rays : (2 * j + 1) * rays]
            uneven = grad[(2 * j + 1) * rays : (2 * j + 2) * rays]
            gnat[seg * rays : (seg + 1) * rays, j * 128 : (j + 1) * 128] = (
                even + pltpu.roll(uneven, 64, 1)
            ).astype(BF16)

    keep = parity_s[...]
    first = lane128 < 64
    for j in range(4):
        pair = jnp.dot(
            order_s[...], gnat[:, j * 128 : (j + 1) * 128], preferred_element_type=F32
        )
        swapped = pltpu.roll(pair, 64, 1)
        gsort[pl.ds(2 * j, sorted_rows, stride=8), :] = jnp.where(first, pair, swapped) * keep
        gsort[pl.ds(2 * j + 1, sorted_rows, stride=8), :] = jnp.where(first, swapped, pair) * keep

    def block(h):
        grads = gsort[h * cap * 8 : (h + 1) * cap * 8, :].astype(BF16)
        return jnp.dot(wturned[h], grads, preferred_element_type=F32)

    half = ny // 2
    a, b = pl.ds(0, half), pl.ds(half, half)
    core, far_a, far_b, left_a, left_b, right_a, right_b = {}, {}, {}, {}, {}, {}, {}
    for j in (2, 1, 3, 0):
        for e in range(ny):
            made = block((NX + j) * ny + e)
            outb[0, j, e] = made[:32]
            outb[1, j, e] = made[32:]
        for q in range(2):
            core[q, j] = copies.start(outb.at[q, j], cbuf.at[q, j], partner)
    for j in (2, 1, 3, 0):
        for e in range(ny):
            made = block(j * ny + e)
            part[0, j, e] = made[:32]
            part[1, j, e] = made[32:]

    def merge(q, j):
        core[q, j].wait_recv()
        part[q, j] = part[q, j] + cbuf[q, j]

    for q in range(2):
        merge(q, 2)
        far_a[q] = copies.start(part.at[q, 2, a], relay_a.at[q], right)
        far_b[q] = copies.start(part.at[q, 2, b], relay_b.at[q], left)
        merge(q, 1)
        left_b[q] = copies.start(part.at[q, 1, b], from_left.at[q, b], right)
        merge(q, 3)
        right_a[q] = copies.start(part.at[q, 3, a], from_right.at[q, a], left)
    for q in range(2):
        far_a[q].wait_recv()
        part[q, 1, a] = part[q, 1, a] + relay_a[q]
        left_a[q] = copies.start(part.at[q, 1, a], from_left.at[q, a], right)
        far_b[q].wait_recv()
        part[q, 3, b] = part[q, 3, b] + relay_b[q]
        right_b[q] = copies.start(part.at[q, 3, b], from_right.at[q, b], left)
        merge(q, 0)
    ys, zs = {}, []
    for q in range(2):
        for copy, side in ((right_a, a), (left_a, a), (left_b, b), (right_b, b)):
            copy[q].wait_recv()
        part[q, 0] = part[q, 0] + from_left[q] + from_right[q]
        for d in near_first(ny):
            ys[q, d] = copies.start(part.at[q, 0, d], ybuf.at[q, ny - d], peers.along_y(d))
    used = pl.ds(0, 32)
    for q in range(2):
        total = part[q, 0, 0]
        for d in near_first(ny):
            ys[q, d].wait_recv()
            total = total + ybuf[q, ny - d]
        zout_ref[q, 0, used] = total
        for d in near_first(nz):
            zs.append(
                copies.start(
                    zout_ref.at[q, 0, used], zout_ref.at[q, nz - d, used], peers.along_z(d)
                )
            )
    for copy in zs:
        copy.wait_recv()
    copies.drain()


def step(nz, ny, work_bricks, slots, *operands):
    bricks, interp = operands[:2]
    segs, rays, _ = interp.shape
    tiles, samples, holders = segs * rays, segs * rays * 8, NC * NX * ny
    cap = 2 * tiles // holders
    total = step_copies(nz, ny)
    vmem = pl.BlockSpec(memory_space=pltpu.VMEM)
    smem = pl.BlockSpec(memory_space=pltpu.SMEM)
    hbm = pl.BlockSpec(memory_space=pltpu.HBM)
    unit = (32, 128)
    every = pltpu.VMEM((2, NX, ny) + unit, F32)
    whole = pltpu.VMEM((2, ny) + unit, F32)
    half = pltpu.VMEM((2, ny // 2) + unit, F32)
    return pl.pallas_call(
        functools.partial(step_kernel, nz, ny),
        out_shape=(
            jax.ShapeDtypeStruct((2, nz, PITCH, 128), F32),
            jax.ShapeDtypeStruct((nz, 8, 128), jnp.int32),
        ),
        in_specs=[smem, smem, vmem] + [hbm] * 7,
        out_specs=(vmem, vmem),
        scratch_shapes=[
            pltpu.VMEM(x.shape, x.dtype)
            for x in (bricks, interp) + operands[2:]
        ]
        + [
            pltpu.VMEM((8, 128), jnp.int32),
            pltpu.VMEM((2 * nz * PITCH, 128), F32),
            pltpu.VMEM((2, nz) + unit, BF16),
            pltpu.VMEM((2, nz) + unit, BF16),
            pltpu.VMEM((holders, 2) + unit, BF16),
            pltpu.VMEM((tiles * 24, 128), F32),
            pltpu.VMEM(((rays + 8) * 8, 128), F32),
            pltpu.VMEM(((rays + 8) * 8, 128), F32),
            pltpu.VMEM((samples, 256), F32),
            pltpu.VMEM((samples, 256), F32),
            pltpu.VMEM((8 * segs * 8, 128), F32),
            pltpu.VMEM((8 * segs * 8, 128), F32),
            pltpu.VMEM((holders * cap, tiles), BF16),
            pltpu.VMEM((holders * cap, 128), F32),
            pltpu.VMEM((holders * cap * 8, 128), F32),
            pltpu.VMEM((holders, 64, cap * 8), BF16),
            pltpu.VMEM((tiles, 512), BF16),
            pltpu.VMEM((holders * cap * 8, 128), F32),
            every,
            every,
            every,
            half,
            half,
            whole,
            whole,
            whole,
            pltpu.SemaphoreType.DMA((7,)),
            pltpu.SemaphoreType.DMA((total,)),
            pltpu.SemaphoreType.DMA((total,)),
        ],
        compiler_params=pltpu.CompilerParams(collective_id=0, has_side_effects=True),
        name="step",
    )(work_bricks, slots, slots, *operands)


def place_kernel(base_ref, reqs_ref, z_ref, out_ref):
    nz = reqs_ref.shape[0]
    own_count = out_ref.shape[0]
    ids = [reqs_ref[e, s : s + 1, :] for s in range(2) for e in range(nz)]
    hit = indicator(jnp.concatenate(ids, axis=0) - base_ref[0] == iota((2 * nz, 128), 1))
    spread = jnp.transpose(hit)[:own_count]
    first = iota((nz, 128), 1) < 64
    for p in range(32):
        at = p // 16 * (nz * PITCH) + p % 16 * 2
        even = z_ref[pl.ds(at, nz, stride=PITCH), :]
        uneven = z_ref[pl.ds(at + 1, nz, stride=PITCH), :]
        rows = jnp.concatenate(
            [
                jnp.where(first, even, pltpu.roll(uneven, 64, 1)),
                jnp.where(first, pltpu.roll(even, 64, 1), uneven),
            ],
            axis=0,
        )
        out_ref[:, p * 128 : (p + 1) * 128] = jnp.dot(
            spread, rows, precision=HIGHEST, preferred_element_type=F32
        )


def place(own_count, base, reqs, zout):
    vmem = pl.BlockSpec(memory_space=pltpu.VMEM)
    return pl.pallas_call(
        place_kernel,
        out_shape=jax.ShapeDtypeStruct((own_count, 4096), F32),
        in_specs=[pl.BlockSpec(memory_space=pltpu.SMEM), vmem, vmem],
        out_specs=vmem,
        name="place",
    )(base, reqs, zout.reshape(-1, 128))


def per_device(
    bricks, work_bricks, interp, tile_slot, spacing, targets, weight_in, weight_mid, weight_out
):
    nz = lax.axis_size("group")
    ny = lax.axis_size("ray") // (NX * NC)
    own_count = bricks.shape[0]
    base = (lax.axis_index("group") * lax.axis_size("ray") + lax.axis_index("ray")) * own_count
    zout, reqs = step(
        nz,
        ny,
        work_bricks,
        tile_slot.T,
        bricks,
        interp.transpose(1, 0, 2),
        weight_in,
        weight_mid,
        weight_out.T,
        spacing.T,
        targets,
    )
    return place(own_count, base.reshape(1), reqs, zout)


def solution(mesh):
    in_specs = (
        P(("group", "ray"), None),
        P("group", "ray"),
        P(("group", "ray"), None, None),
        P(("group", "ray"), None),
        P(("group", "ray"), None),
        P(None, ("group", "ray")),
        P(),
        P(),
        P(),
    )
    out_specs = P(("group", "ray"), None)
    return jax.shard_map(
        per_device, mesh=mesh, in_specs=in_specs, out_specs=out_specs, check_vma=False
    )
```

time: 439 us -> 75.9 us (0.17)
  the two profiles are of different devices: /device:TPU:1 before, /device:TPU:2 now
where the time goes in v3:
time: 75.9 us; the launch traced here: 75.8 us
  Pallas kernels  75.7 us (100%)
    pallas_call x1, Pallas kernels, step(): pl.pallas_call(functools.partial(step_kernel, nz, ny), out_shape=(jax.Sha...  73.2 us
    pallas_call x1, Pallas kernels, place(): pl.pallas_call(place_kernel, out_shape=jax.ShapeDtypeStruct((own_count, 4...  2.58 us

profile of v3, /device:TPU:2, one launch (start us, length us, event | category | flops | bytes accessed | tf_op | source)
XLA Modules:
  0.0 75.8 jit_solution(14822490967083746044)
XLA Ops:
  0.0 73.2 %step.1 = (f32[2,8,40,128]{3,2,1,0:T(8,128)}, s32[8,8,128]{2,1,0:T(8,128)}) custom-call(s32[1,2]{1,0:T(1,128)} %wb_ref.1, s32[5,64]{1,0:T(8,128)} %bitcast.9, s32[5,64]{1,0:T(8,128)} %bitcast.10, bf16[32,4096]{1,0:T(8,128)(2,1)} %bricks_hbm.1, bf16[5,64,512]{2,1,0:T(8,128)(2,1)} %bitcast.6, bf16[64,256]{1,0:T(8,128)(2,1)} %win_hbm.1, ...), custom_call_target="tpu_custom_call" | custom-call | tf_op jit(solution)/shard_map/step/pallas_call | solution.py:494
  73.2 2.6 %place.1 = f32[32,4096]{1,0:T(8,128)} custom-call(s32[1]{0:T(128)} %bitcast.base_ref, s32[8,8,128]{2,1,0:T(8,128)} %get-tuple-element.7.reqs_ref, f32[640,128]{1,0:T(8,128)} %bitcast.7), custom_call_target="tpu_custom_call" | custom-call | tf_op jit(solution)/shard_map/place/pallas_call | solution.py:567

commit v4 on v3

--- a/solution.py
+++ b/solution.py
@@ -13,6 +13,7 @@
 NX = 4
 NC = 2
 PITCH = 40
+SLICES = 4
 HIGHEST = lax.Precision.HIGHEST
 
 
@@ -114,7 +115,7 @@
 
 def step_copies(nz, ny):
     fetched = 2 * (nz - 1) + (nz - 1) + 2 * (ny - 1) + 3 * ny + 4 * ny
-    return fetched + 2 * (4 + 6 + (ny - 1) + (nz - 1))
+    return fetched + SLICES * (4 + 6 + (ny - 1) + (nz - 1))
 
 
 def step_kernel(
@@ -130,8 +131,7 @@
     wout_hbm,
     spacing_hbm,
     targets_hbm,
-    zout_ref,
-    reqs_ref,
+    out_hbm,
     bricks_ref,
     interp_ref,
     win_ref,
@@ -139,6 +139,11 @@
     wout_ref,
     spacing_ref,
     targets_ref,
+    reqs_ref,
+    out_ref,
+    spread_s,
+    zbuf,
+    save_sems,
     mine,
     picks,
     sendb,
@@ -265,7 +270,9 @@
     for s in range(2):
         ids = jnp.concatenate([reqs_ref[e, s : s + 1, :] for e in range(nz)], axis=0)
         rows.append(indicator(ids - base == iota((nz, 128), 1)))
-    choose = jnp.concatenate(rows, axis=0)[:, :own_count].astype(BF16)
+    choose = jnp.concatenate(rows, axis=0)
+    spread_s[...] = jnp.transpose(choose)[:own_count]
+    choose = choose[:, :own_count].astype(BF16)
     picked = jnp.dot(choose, bricks_ref[...], preferred_element_type=F32)
     gives = {}
     for s in range(2):
@@ -324,24 +331,22 @@
     wmid = wmid_ref[...] * 0.5
     wout = jnp.concatenate([wout_ref[...].astype(F32), jnp.zeros((4, 256), F32)], axis=0).astype(BF16)
     win_wide = jnp.concatenate([win.astype(F32), jnp.zeros((64, 256), F32)], axis=0).astype(BF16)
-    unroll = 16
-    for seg in range(segs):
-
-        @pl.loop(0, rays // unroll)
-        def _(group):
-            for u in range(unroll):
-                r = group * unroll + u
-                name = slots_ref[seg, r]
-                brick = gs[name >> 1, name & 1]
-                at = pl.multiple_of((seg * rays + r) * 24, 8)
-                weights = wc[pl.ds(at, 16), :][:, :32].astype(BF16)
-                made = jnp.dot(weights, brick, preferred_element_type=F32)
-                feat_a[pl.ds(r, 8, stride=pitch), :] = made[:8]
-                feat_b[pl.ds(r, 8, stride=pitch), :] = made[8:]
-
+
+    def tiles_of(seg):
+        for r in range(rays):
+            name = slots_ref[seg, r]
+            brick = gs[name >> 1, name & 1]
+            at = (seg * rays + r) * 24
+            weights = wc[at : at + 16, :][:, :32].astype(BF16)
+            made = jnp.dot(weights, brick, preferred_element_type=F32)
+            feat_a[seg % 2, pl.ds(r, 8, stride=pitch), :] = made[:8]
+            feat_b[seg % 2, pl.ds(r, 8, stride=pitch), :] = made[8:]
+
+    def forward(seg):
         rows = pl.ds(seg * chunk, chunk)
-        features = (feat_a[...] + pltpu.roll(feat_b[...], 64, 1)).reshape(8, pitch, 128)
-        features = features[:, :rays].reshape(chunk, 128)[:, :64].astype(BF16)
+        features = feat_a[seg % 2] + pltpu.roll(feat_b[seg % 2], 64, 1)
+        features = features.reshape(8, pitch, 128)[:, :rays].reshape(chunk, 128)
+        features = features[:, :64].astype(BF16)
         act, slope_a[rows, :] = silu_of_half(jnp.dot(features, win, preferred_element_type=F32))
         act, slope_b[rows, :] = silu_of_half(
             jnp.dot(act.astype(BF16), wmid, preferred_element_type=F32)
@@ -354,6 +359,12 @@
             at = i * rays
             raw_s[pl.ds(seg * 8 + i, 8, stride=steps), :] = raw[:, at : at + 128]
             raw_s[pl.ds(seg * 8 + i + 1, 8, stride=steps), :] = turned[:, at : at + 128]
+
+    tiles_of(0)
+    for seg in range(segs):
+        if seg + 1 < segs:
+            tiles_of(seg + 1)
+        forward(seg)
 
     spacing = spacing_ref[...]
     k0, k1 = iota((steps, steps), 0), iota((steps, steps), 1)
@@ -417,27 +428,28 @@
         grads = gsort[h * cap * 8 : (h + 1) * cap * 8, :].astype(BF16)
         return jnp.dot(wturned[h], grads, preferred_element_type=F32)
 
+    def cut(made, to, j, e):
+        for q in range(SLICES):
+            to[q, j, e] = made[q * depth : (q + 1) * depth]
+
+    depth = 64 // SLICES
     half = ny // 2
     a, b = pl.ds(0, half), pl.ds(half, half)
     core, far_a, far_b, left_a, left_b, right_a, right_b = {}, {}, {}, {}, {}, {}, {}
     for j in (2, 1, 3, 0):
         for e in range(ny):
-            made = block((NX + j) * ny + e)
-            outb[0, j, e] = made[:32]
-            outb[1, j, e] = made[32:]
-        for q in range(2):
+            cut(block((NX + j) * ny + e), outb, j, e)
+        for q in range(SLICES):
             core[q, j] = copies.start(outb.at[q, j], cbuf.at[q, j], partner)
     for j in (2, 1, 3, 0):
         for e in range(ny):
-            made = block(j * ny + e)
-            part[0, j, e] = made[:32]
-            part[1, j, e] = made[32:]
+            cut(block(j * ny + e), part, j, e)
 
     def merge(q, j):
         core[q, j].wait_recv()
         part[q, j] = part[q, j] + cbuf[q, j]
 
-    for q in range(2):
+    def first_leg(q):
         merge(q, 2)
         far_a[q] = copies.start(part.at[q, 2, a], relay_a.at[q], right)
         far_b[q] = copies.start(part.at[q, 2, b], relay_b.at[q], left)
@@ -445,7 +457,8 @@
         left_b[q] = copies.start(part.at[q, 1, b], from_left.at[q, b], right)
         merge(q, 3)
         right_a[q] = copies.start(part.at[q, 3, a], from_right.at[q, a], left)
-    for q in range(2):
+
+    def second_leg(q):
         far_a[q].wait_recv()
         part[q, 1, a] = part[q, 1, a] + relay_a[q]
         left_a[q] = copies.start(part.at[q, 1, a], from_left.at[q, a], right)
@@ -453,28 +466,61 @@
         part[q, 3, b] = part[q, 3, b] + relay_b[q]
         right_b[q] = copies.start(part.at[q, 3, b], from_right.at[q, b], left)
         merge(q, 0)
-    ys, zs = {}, []
-    for q in range(2):
-        for copy, side in ((right_a, a), (left_a, a), (left_b, b), (right_b, b)):
+
+    ys, zs = {}, {}
+
+    def along_columns(q):
+        for copy in (right_a, left_a, left_b, right_b):
             copy[q].wait_recv()
         part[q, 0] = part[q, 0] + from_left[q] + from_right[q]
         for d in near_first(ny):
             ys[q, d] = copies.start(part.at[q, 0, d], ybuf.at[q, ny - d], peers.along_y(d))
-    used = pl.ds(0, 32)
-    for q in range(2):
+
+    used = pl.ds(0, depth)
+
+    def across_groups(q):
         total = part[q, 0, 0]
         for d in near_first(ny):
             ys[q, d].wait_recv()
             total = total + ybuf[q, ny - d]
-        zout_ref[q, 0, used] = total
+        zbuf[q, 0, used] = total
         for d in near_first(nz):
-            zs.append(
-                copies.start(
-                    zout_ref.at[q, 0, used], zout_ref.at[q, nz - d, used], peers.along_z(d)
-                )
+            zs[q, d] = copies.start(
+                zbuf.at[q, 0, used], zbuf.at[q, nz - d, used], peers.along_z(d)
             )
-    for copy in zs:
-        copy.wait_recv()
+
+    saves = []
+    left_side = iota((nz, 128), 1) < 64
+
+    def land(q):
+        for d in near_first(nz):
+            zs[q, d].wait_recv()
+        for v in range(0, depth, 2):
+            even = jnp.concatenate([zbuf[q, e, v : v + 1] for e in range(nz)], axis=0)
+            uneven = jnp.concatenate([zbuf[q, e, v + 1 : v + 2] for e in range(nz)], axis=0)
+            rows = jnp.concatenate(
+                [
+                    jnp.where(left_side, even, pltpu.roll(uneven, 64, 1)),
+                    jnp.where(left_side, pltpu.roll(even, 64, 1), uneven),
+                ],
+                axis=0,
+            )
+            at = (q * depth + v) * 64
+            out_ref[:, at : at + 128] = jnp.dot(
+                spread_s[...], rows, precision=HIGHEST, preferred_element_type=F32
+            )
+        lanes = pl.ds(q * depth * 64, depth * 64)
+        saves.append(
+            pltpu.make_async_copy(out_ref.at[:, lanes], out_hbm.at[:, lanes], save_sems.at[q])
+        )
+        saves[q].start()
+
+    stages = (first_leg, second_leg, along_columns, across_groups, land)
+    for stage in stages:
+        for q in range(SLICES):
+            stage(q)
+    for save in saves:
+        save.wait()
     copies.drain()
 
 
@@ -488,30 +534,33 @@
     smem = pl.BlockSpec(memory_space=pltpu.SMEM)
     hbm = pl.BlockSpec(memory_space=pltpu.HBM)
     unit = (32, 128)
-    every = pltpu.VMEM((2, NX, ny) + unit, F32)
-    whole = pltpu.VMEM((2, ny) + unit, F32)
-    half = pltpu.VMEM((2, ny // 2) + unit, F32)
+    depth = 64 // SLICES
+    every = pltpu.VMEM((SLICES, NX, ny, depth, 128), F32)
+    whole = pltpu.VMEM((SLICES, ny, depth, 128), F32)
+    half = pltpu.VMEM((SLICES, ny // 2, depth, 128), F32)
     return pl.pallas_call(
         functools.partial(step_kernel, nz, ny),
-        out_shape=(
-            jax.ShapeDtypeStruct((2, nz, PITCH, 128), F32),
-            jax.ShapeDtypeStruct((nz, 8, 128), jnp.int32),
-        ),
+        out_shape=jax.ShapeDtypeStruct(bricks.shape, F32),
         in_specs=[smem, smem, vmem] + [hbm] * 7,
-        out_specs=(vmem, vmem),
+        out_specs=hbm,
         scratch_shapes=[
             pltpu.VMEM(x.shape, x.dtype)
             for x in (bricks, interp) + operands[2:]
         ]
         + [
+            pltpu.VMEM((nz, 8, 128), jnp.int32),
+            pltpu.VMEM(bricks.shape, F32),
+            pltpu.VMEM((bricks.shape[0], 2 * nz), F32),
+            pltpu.VMEM((SLICES, nz, depth + 8, 128), F32),
+            pltpu.SemaphoreType.DMA((SLICES,)),
             pltpu.VMEM((8, 128), jnp.int32),
             pltpu.VMEM((2 * nz * PITCH, 128), F32),
             pltpu.VMEM((2, nz) + unit, BF16),
             pltpu.VMEM((2, nz) + unit, BF16),
             pltpu.VMEM((holders, 2) + unit, BF16),
             pltpu.VMEM((tiles * 24, 128), F32),
-            pltpu.VMEM(((rays + 8) * 8, 128), F32),
-            pltpu.VMEM(((rays + 8) * 8, 128), F32),
+            pltpu.VMEM((2, (rays + 8) * 8, 128), F32),
+            pltpu.VMEM((2, (rays + 8) * 8, 128), F32),
             pltpu.VMEM((samples, 256), F32),
             pltpu.VMEM((samples, 256), F32),
             pltpu.VMEM((8 * segs * 8, 128), F32),
@@ -539,48 +588,12 @@
     )(work_bricks, slots, slots, *operands)
 
 
-def place_kernel(base_ref, reqs_ref, z_ref, out_ref):
-    nz = reqs_ref.shape[0]
-    own_count = out_ref.shape[0]
-    ids = [reqs_ref[e, s : s + 1, :] for s in range(2) for e in range(nz)]
-    hit = indicator(jnp.concatenate(ids, axis=0) - base_ref[0] == iota((2 * nz, 128), 1))
-    spread = jnp.transpose(hit)[:own_count]
-    first = iota((nz, 128), 1) < 64
-    for p in range(32):
-        at = p // 16 * (nz * PITCH) + p % 16 * 2
-        even = z_ref[pl.ds(at, nz, stride=PITCH), :]
-        uneven = z_ref[pl.ds(at + 1, nz, stride=PITCH), :]
-        rows = jnp.concatenate(
-            [
-                jnp.where(first, even, pltpu.roll(uneven, 64, 1)),
-                jnp.where(first, pltpu.roll(even, 64, 1), uneven),
-            ],
-            axis=0,
-        )
-        out_ref[:, p * 128 : (p + 1) * 128] = jnp.dot(
-            spread, rows, precision=HIGHEST, preferred_element_type=F32
-        )
-
-
-def place(own_count, base, reqs, zout):
-    vmem = pl.BlockSpec(memory_space=pltpu.VMEM)
-    return pl.pallas_call(
-        place_kernel,
-        out_shape=jax.ShapeDtypeStruct((own_count, 4096), F32),
-        in_specs=[pl.BlockSpec(memory_space=pltpu.SMEM), vmem, vmem],
-        out_specs=vmem,
-        name="place",
-    )(base, reqs, zout.reshape(-1, 128))
-
-
 def per_device(
     bricks, work_bricks, interp, tile_slot, spacing, targets, weight_in, weight_mid, weight_out
 ):
     nz = lax.axis_size("group")
     ny = lax.axis_size("ray") // (NX * NC)
-    own_count = bricks.shape[0]
-    base = (lax.axis_index("group") * lax.axis_size("ray") + lax.axis_index("ray")) * own_count
-    zout, reqs = step(
+    return step(
         nz,
         ny,
         work_bricks,
@@ -593,7 +606,6 @@
         spacing.T,
         targets,
     )
-    return place(own_count, base.reshape(1), reqs, zout)
 
 
 def solution(mesh):

time: 75.9 us -> 71.2 us (0.938)
  the two profiles are of different devices: /device:TPU:2 before, /device:TPU:1 now
where the time goes in v4:
time: 71.2 us; the launch traced here: 70.3 us
  Pallas kernels  68.4 us (96%)
  local copies, waits for them, and re-layouts  1.87 us (3%)
    pallas_call x1, Pallas kernels, step(): pl.pallas_call(functools.partial(step_kernel, nz, ny), out_shape=jax.Shap...  68.4 us
    unnamed x1, local copies, waits for them, and re-layouts  1.87 us

profile of v4, /device:TPU:1, one launch (start us, length us, event | category | flops | bytes accessed | tf_op | source)
XLA Modules:
  0.0 70.3 jit_solution(1536089824129939974)
XLA Ops:
  0.0 68.4 %step.1 = f32[32,4096]{1,0:T(8,128)} custom-call(s32[1,2]{1,0:T(1,128)} %wb_ref.1, s32[5,64]{1,0:T(8,128)} %bitcast.6, s32[5,64]{1,0:T(8,128)} %bitcast.7, bf16[32,4096]{1,0:T(8,128)(2,1)} %bricks_hbm.1, bf16[5,64,512]{2,1,0:T(8,128)(2,1)} %bitcast.4, bf16[64,256]{1,0:T(8,128)(2,1)} %win_hbm.1, bf16[256,256]{1,0:T(8,128)(2,1)} %wmid_hbm.1, ...), custom_call_target="tpu_custom_call" | custom-call | tf_op jit(solution)/shard_map/step/pallas_call | solution.py:541
  68.4 1.9 %copy.11 = f32[32,4096]{1,0:T(8,128)} copy(f32[32,4096]{1,0:T(8,128)} %step.1) | data formatting | bytes 1048576

commit v5 on v4

--- a/solution.py
+++ b/solution.py
@@ -45,8 +45,8 @@
         return {"ray": ray_of(self.y, self.x, 1 - self.c)}
 
     def everybody(self):
-        out = [self.along_z(d) for d in range(1, self.nz)]
-        out += [self.along_y(d) for d in range(1, self.ny)]
+        out = [self.along_z(d) for d in far_first(self.nz)]
+        out += [self.along_y(d) for d in far_first(self.ny)]
         return out + [self.along_x(d) for d in range(1, NX)] + [self.partner()]
 
     def greet(self):
@@ -83,15 +83,15 @@
     def drain(self):
         for copy in self.live:
             copy.wait_send()
+        self.live = []
+
+
+def far_first(n):
+    return sorted(range(1, n), key=lambda d: -min(d, n - d))
 
 
 def near_first(n):
-    out = []
-    for d in range(1, n // 2 + 1):
-        out.append(d)
-        if n - d != d:
-            out.append(n - d)
-    return out
+    return far_first(n)[::-1]
 
 
 def logistic(x):
@@ -115,15 +115,14 @@
 
 def step_copies(nz, ny):
     fetched = 2 * (nz - 1) + (nz - 1) + 2 * (ny - 1) + 3 * ny + 4 * ny
-    return fetched + SLICES * (4 + 6 + (ny - 1) + (nz - 1))
+    return fetched + SLICES * (4 + 6 + (ny - 1) + (nz - 1)) - 3
 
 
 def step_kernel(
     nz,
     ny,
-    wb_ref,
-    slots_ref,
-    slotv_ref,
+    wb_hbm,
+    slots_hbm,
     bricks_hbm,
     interp_hbm,
     win_hbm,
@@ -139,6 +138,9 @@
     wout_ref,
     spacing_ref,
     targets_ref,
+    wb_ref,
+    slots_ref,
+    slotv_ref,
     reqs_ref,
     out_ref,
     spread_s,
@@ -170,6 +172,8 @@
     from_left,
     from_right,
     ybuf,
+    columns,
+    across,
     load_sems,
     send_sems,
     recv_sems,
@@ -185,10 +189,14 @@
     steps = segs * 8
     pitch = rays + 8
     own_count = bricks_ref.shape[0]
+    barrier = peers.greet()
     loads = []
     for n, (src, dst) in enumerate(
         (
+            (wb_hbm, wb_ref),
+            (slots_hbm, slotv_ref),
             (interp_hbm, interp_ref),
+            (slots_hbm, slots_ref),
             (bricks_hbm, bricks_ref),
             (win_hbm, win_ref),
             (wmid_hbm, wmid_ref),
@@ -199,10 +207,11 @@
     ):
         loads.append(pltpu.make_async_copy(src, dst, load_sems.at[n]))
         loads[n].start()
+    loads[0].wait()
     ask = jnp.where(iota(mine.shape, 0) == 0, wb_ref[0, 0], wb_ref[0, 1])
     mine[...] = ask
     reqs_ref[0] = ask
-    barrier = peers.greet()
+    loads[1].wait()
 
     slot = slotv_ref[...]
     holder = slot // 2
@@ -228,7 +237,7 @@
     perm = indicator(
         (dst // 128 == (src // 64) * 2 + voxel % 2) & (dst % 128 == voxel // 2), BF16
     )
-    loads[0].wait()
+    loads[2].wait()
     for seg in range(segs):
         for j in range(4):
             moved = jnp.dot(
@@ -241,7 +250,7 @@
                         :, blk * 128 : (blk + 1) * 128
                     ]
     barrier()
-    asks = [copies.start(mine, reqs_ref.at[nz - d], peers.along_z(d)) for d in near_first(nz)]
+    asks = [copies.start(mine, reqs_ref.at[nz - d], peers.along_z(d)) for d in far_first(nz)]
 
     natural = interp_ref[...].reshape(tiles, 512)
     ordered = jnp.dot(order_s[...], natural, preferred_element_type=F32)
@@ -261,7 +270,7 @@
             block = wsort[h * cap * 8 : (h + 1) * cap * 8, :]
             wturned[h] = jnp.transpose(block)[:64].astype(BF16)
 
-    for load in loads[1:]:
+    for load in loads[3:]:
         load.wait()
     for copy in asks:
         copy.wait_recv()
@@ -282,7 +291,7 @@
             ]
         rows = picks[s * nz * PITCH : (s + 1) * nz * PITCH, :].reshape(nz, PITCH, 128)
         sendb[s] = rows[:, :32].astype(BF16)
-        for d in near_first(nz):
+        for d in far_first(nz):
             gives[s, d] = copies.start(sendb.at[s, d], arrived.at[s, nz - d], peers.along_z(d))
     turn(0, holders // 2)
     right, far, left = (peers.along_x(d) for d in (1, 2, 3))
@@ -301,7 +310,7 @@
 
     def along_row(e):
         at = unit(peers.c, 0, e)
-        for j, device in ((3, right), (1, left), (2, far)):
+        for j, device in ((2, far), (3, right), (1, left)):
             hops[j, e] = copies.start(gs.at[at], gs.at[at], device)
         to_core(0, e)
 
@@ -312,7 +321,7 @@
             held = held + arrived[s, nz - d].astype(F32)
         at = unit(peers.c, 0, 0)
         gs[at, s] = held.astype(BF16)
-        for d in near_first(ny):
+        for d in far_first(ny):
             spread[s, ny - d] = copies.start(gs.at[at, s], gs.at[at, s], peers.along_y(d))
     along_row(0)
     turn(holders // 2, holders)
@@ -467,24 +476,46 @@
         right_b[q] = copies.start(part.at[q, 3, b], from_right.at[q, b], left)
         merge(q, 0)
 
-    ys, zs = {}, {}
+    xs, ys, zs = {}, {}, {}
 
     def along_columns(q):
         for copy in (right_a, left_a, left_b, right_b):
             copy[q].wait_recv()
         part[q, 0] = part[q, 0] + from_left[q] + from_right[q]
+        for d in far_first(ny):
+            ys[q, d] = copies.start(part.at[q, 0, d], ybuf.at[q, ny - d], peers.along_y(d))
+
+    used = pl.ds(0, depth)
+
+    last = SLICES - 1
+
+    def columns_first():
+        for j in (2, 1, 3, 0):
+            merge(last, j)
+        for d in far_first(ny):
+            ys[last, d] = copies.start(
+                part.at[last, :, d], columns.at[ny - d], peers.along_y(d)
+            )
+
+    def rows_second():
         for d in near_first(ny):
-            ys[q, d] = copies.start(part.at[q, 0, d], ybuf.at[q, ny - d], peers.along_y(d))
-
-    used = pl.ds(0, depth)
+            ys[last, d].wait_recv()
+            part[last, :, 0] = part[last, :, 0] + columns[ny - d]
+        for j in (2, 1, 3):
+            xs[j] = copies.start(part.at[last, j, 0], across.at[NX - j], peers.along_x(j))
 
     def across_groups(q):
         total = part[q, 0, 0]
-        for d in near_first(ny):
-            ys[q, d].wait_recv()
-            total = total + ybuf[q, ny - d]
+        if q == last:
+            for j in (1, 3, 2):
+                xs[j].wait_recv()
+                total = total + across[NX - j]
+        else:
+            for d in near_first(ny):
+                ys[q, d].wait_recv()
+                total = total + ybuf[q, ny - d]
         zbuf[q, 0, used] = total
-        for d in near_first(nz):
+        for d in far_first(nz):
             zs[q, d] = copies.start(
                 zbuf.at[q, 0, used], zbuf.at[q, nz - d, used], peers.along_z(d)
             )
@@ -515,10 +546,27 @@
         )
         saves[q].start()
 
-    stages = (first_leg, second_leg, along_columns, across_groups, land)
-    for stage in stages:
-        for q in range(SLICES):
-            stage(q)
+    sent, copies.live = copies.live, []
+    first_leg(0)
+    columns_first()
+    for q in range(1, last):
+        first_leg(q)
+    for copy in sent:
+        copy.wait_send()
+    for q in range(last):
+        second_leg(q)
+    for q in range(last - 1):
+        along_columns(q)
+    rows_second()
+    along_columns(last - 1)
+    sent, copies.live = copies.live, []
+    for q in range(last):
+        across_groups(q)
+    for copy in sent:
+        copy.wait_send()
+    across_groups(last)
+    for q in range(SLICES):
+        land(q)
     for save in saves:
         save.wait()
     copies.drain()
@@ -530,8 +578,6 @@
     tiles, samples, holders = segs * rays, segs * rays * 8, NC * NX * ny
     cap = 2 * tiles // holders
     total = step_copies(nz, ny)
-    vmem = pl.BlockSpec(memory_space=pltpu.VMEM)
-    smem = pl.BlockSpec(memory_space=pltpu.SMEM)
     hbm = pl.BlockSpec(memory_space=pltpu.HBM)
     unit = (32, 128)
     depth = 64 // SLICES
@@ -541,13 +587,16 @@
     return pl.pallas_call(
         functools.partial(step_kernel, nz, ny),
         out_shape=jax.ShapeDtypeStruct(bricks.shape, F32),
-        in_specs=[smem, smem, vmem] + [hbm] * 7,
+        in_specs=[hbm] * 9,
         out_specs=hbm,
         scratch_shapes=[
             pltpu.VMEM(x.shape, x.dtype)
             for x in (bricks, interp) + operands[2:]
         ]
         + [
+            pltpu.SMEM(work_bricks.shape, jnp.int32),
+            pltpu.SMEM(slots.shape, jnp.int32),
+            pltpu.VMEM(slots.shape, jnp.int32),
             pltpu.VMEM((nz, 8, 128), jnp.int32),
             pltpu.VMEM(bricks.shape, F32),
             pltpu.VMEM((bricks.shape[0], 2 * nz), F32),
@@ -579,13 +628,15 @@
             whole,
             whole,
             whole,
-            pltpu.SemaphoreType.DMA((7,)),
+            pltpu.VMEM((ny, NX, depth, 128), F32),
+            pltpu.VMEM((NX, depth, 128), F32),
+            pltpu.SemaphoreType.DMA((10,)),
             pltpu.SemaphoreType.DMA((total,)),
             pltpu.SemaphoreType.DMA((total,)),
         ],
         compiler_params=pltpu.CompilerParams(collective_id=0, has_side_effects=True),
         name="step",
-    )(work_bricks, slots, slots, *operands)
+    )(work_bricks, slots, *operands)
 
 
 def per_device(

time: 71.2 us -> 67.9 us (0.954)
  Pallas kernels: 68.4 us -> 65.8 us
    pallas_call x1, Pallas kernels: 68.4 us -> 65.8 us  [step(): pl.pallas_call(functools.partial(step_kernel, nz, ny), out_shape=jax.Shap...]
where the time goes in v5:
time: 67.9 us; the launch traced here: 67.7 us
  Pallas kernels  65.8 us (97%)
  local copies, waits for them, and re-layouts  1.87 us (3%)
    pallas_call x1, Pallas kernels, step(): pl.pallas_call(functools.partial(step_kernel, nz, ny), out_shape=jax.Shap...  65.8 us
    unnamed x1, local copies, waits for them, and re-layouts  1.87 us

profile of v5, /device:TPU:1, one launch (start us, length us, event | category | flops | bytes accessed | tf_op | source)
XLA Modules:
  0.0 67.7 jit_solution(12853543094145607500)
XLA Ops:
  0.0 65.8 %step.1 = f32[32,4096]{1,0:T(8,128)} custom-call(s32[1,2]{1,0:T(1,128)} %wb_hbm.1, s32[5,64]{1,0:T(8,128)} %bitcast.6, bf16[32,4096]{1,0:T(8,128)(2,1)} %bricks_hbm.1, bf16[5,64,512]{2,1,0:T(8,128)(2,1)} %bitcast.4, bf16[64,256]{1,0:T(8,128)(2,1)} %win_hbm.1, bf16[256,256]{1,0:T(8,128)(2,1)} %wmid_hbm.1, bf16[4,256]{1,0:T(4,128)(2,1)} %bitcast.7, ...), custom_call_target="tpu_custom_call" | custom-call | tf_op jit(solution)/shard_map/step/pallas_call | solution.py:587
  65.8 1.9 %copy.11 = f32[32,4096]{1,0:T(8,128)} copy(f32[32,4096]{1,0:T(8,128)} %step.1) | data formatting | bytes 1048576
